TPU v7x, 32 devices: a whole 2x2x4 slice. The times are simulated.
32 devices in a mesh: dp: 16 (over z, y, core), fsdp: 2 (over x).
Axes of the slice: x: 2, y: 2, z: 4, core: 2. Of those that a mesh axis runs over, the one named last changes fastest.
Arguments:
- tokens: bfloat16 [8192, 1024], P(('dp', 'fsdp')), may hold values from -6 to 6
- image_ids: int32 [8192], P(('dp', 'fsdp')), may hold values from 0 to 5, as said below
- pad_mask: int32 [8192], P(('dp', 'fsdp')), may hold values from 0 to 1, as said below
- cotangent: bfloat16 [8192, 1024], P(('dp', 'fsdp')), may hold values from -6 to 6
- w_qkv: bfloat16 [2, 1024, 3072], P(None, 'fsdp'), may hold values from -0.1875 to 0.1875
- w_out: bfloat16 [2, 1024, 1024], P(None, 'fsdp'), may hold values from -6 to 6
- w_fc1: bfloat16 [2, 1024, 4096], P(None, 'fsdp'), may hold values from -0.1875 to 0.1875
- w_fc2: bfloat16 [2, 4096, 1024], P(None, 'fsdp'), may hold values from -0.09375 to 0.09375
- b_fc1: bfloat16 [2, 4096], P(None, 'fsdp'), may hold values from -3 to 3
- proj_bias: bfloat16 [2, 3, 1024], P(None, None, 'fsdp'), may hold values from -2 to 2
- value_bias: bfloat16 [2, 1024], P(None, 'fsdp'), may hold values from -0.3984375 to 0.3984375
- ln_gain: bfloat16 [2, 2, 1024], P(None, None, 'fsdp'), may hold values from 0.5 to 1.5
- ln_shift: bfloat16 [2, 2, 1024], P(None, None, 'fsdp'), may hold values from -1.1953125 to 1.1953125
- layer_scale: bfloat16 [2, 2, 1024], P(None, None, 'fsdp'), may hold values from 0.25 to 1
Outputs:
- output: bfloat16 [8192, 1024], P(('dp', 'fsdp'))
- input_grad: bfloat16 [8192, 1024], P(('dp', 'fsdp'))
- grad_w_qkv: float32 [2, 1024, 3072], P(None, 'fsdp')
- grad_w_out: float32 [2, 1024, 1024], P(None, 'fsdp')
- grad_w_fc1: float32 [2, 1024, 4096], P(None, 'fsdp')
- grad_w_fc2: float32 [2, 4096, 1024], P(None, 'fsdp')
- grad_b_fc1: float32 [2, 4096], P(None, 'fsdp')
- grad_proj_bias: float32 [2, 3, 1024], P(None, None, 'fsdp')
- grad_value_bias: float32 [2, 1024], P(None, 'fsdp')
- grad_ln_gain: float32 [2, 2, 1024], P(None, None, 'fsdp')
- grad_ln_shift: float32 [2, 2, 1024], P(None, None, 'fsdp')
- grad_layer_scale: float32 [2, 2, 1024], P(None, None, 'fsdp')
Inputs may be any that keep to these rules, and one draw needn't show every extreme that they name: `image_ids`: images are runs of exactly 1370 consecutive tokens numbered 0 to 4 in stream order; runs of padding tokens lie between some of them and after them and carry the number 5. pad_mask is 1 exactly on the tokens whose image number is below 5.
All inputs are finite; a program needn't handle non-finite values.
Results may differ from a plain program's by a relative error of at most 0.017.
Values may be sent and summed in bfloat16 or wider, within the bound.
No kernel may reach another device: no remote copies, remote signals or barrier semaphores. Data moves between devices by JAX's collectives and lax.ppermute only.
A program may use at most 320 MiB of HBM per device.

v0:
```python
import jax
import jax.numpy as jnp
from jax import lax
from jax.sharding import PartitionSpec as P

HD = 64
LAYERS = 2
REACH = 6


def passed_along(x, axis, by):
    length = lax.axis_size(axis)
    pairs = [(i, i + by) for i in range(length) if 0 <= i + by < length]
    return lax.ppermute(x, axis, pairs)


def layer_norm(values, gain_row, shift_row):
    centre = values - jnp.mean(values, axis=-1, keepdims=True)
    spread = jnp.mean(centre * centre, axis=-1, keepdims=True)
    return centre * lax.rsqrt(spread + 1e-06) * gain_row + shift_row


def gelu_exact(values):
    return jax.nn.gelu(values, approximate=False)


def contract_rows(left_side, right_side):
    return lax.dot_general(
        left_side, right_side, (((0,), (0,)), ((), ())), preferred_element_type=jnp.float32
    )


def times_transposed(left_side, right_side):
    return lax.dot_general(
        left_side, right_side, (((1,), (1,)), ((), ())), preferred_element_type=jnp.float32
    )


def split_heads(matrix):
    return jnp.moveaxis(matrix.reshape(matrix.shape[0], -1, 4, HD), 1, 0)


def join_heads(blocks):
    return jnp.moveaxis(blocks, 0, 1).reshape(blocks.shape[1], -1)


def image_window(image_ids, pad_mask):
    stacked = jnp.stack([image_ids, pad_mask])
    pieces = []
    for offset in range(2 * REACH + 1):
        if offset == REACH:
            pieces.append(stacked)
        else:
            pieces.append(passed_along(stacked, ("dp", "fsdp"), REACH - offset))
    window = jnp.concatenate(pieces, axis=1)
    return (window[0], window[1])


def key_window_of(key_rows, value_rows):
    stacked = jnp.stack([key_rows, value_rows])
    pieces = []
    for offset in range(2 * REACH + 1):
        if offset == REACH:
            pieces.append(stacked)
        else:
            pieces.append(passed_along(stacked, ("dp", "fsdp"), REACH - offset))
    window = jnp.concatenate(pieces, axis=1)
    return (window[0], window[1])


def return_grads(grad_key_window, grad_value_window, row_count):
    stacked = jnp.stack([grad_key_window, grad_value_window])
    local_sum = stacked[:, REACH * row_count : (REACH + 1) * row_count]
    for offset in range(2 * REACH + 1):
        if offset != REACH:
            piece = stacked[:, offset * row_count : (offset + 1) * row_count]
            local_sum = local_sum + passed_along(
                piece.astype(jnp.bfloat16), ("dp", "fsdp"), offset - REACH
            ).astype(piece.dtype)
    return (local_sum[0], local_sum[1])


def attend(queries, key_window, value_window, allowed):

    def group_step(operands):
        query_grp, key_grp, value_grp = operands
        scores = (
            jnp.einsum("qhd,khd->hqk", query_grp, key_grp, preferred_element_type=jnp.float32)
            * 0.125
        )
        scores = jnp.where(allowed[None], scores, -1e30)
        row_top = jnp.max(scores, axis=-1, keepdims=True)
        exponent = jnp.exp(scores - row_top)
        row_total = jnp.sum(exponent, axis=-1, keepdims=True)
        soft_probs = (exponent / row_total).astype(jnp.bfloat16)
        mixed_heads = jnp.einsum(
            "hqk,khd->qhd", soft_probs, value_grp, preferred_element_type=jnp.float32
        )
        return (mixed_heads, (row_top + jnp.log(row_total))[..., 0])

    mixed_heads, log_total = lax.map(
        group_step, (split_heads(queries), split_heads(key_window), split_heads(value_window))
    )
    return (join_heads(mixed_heads), log_total)


def attend_back(queries, key_window, value_window, allowed, log_total, grad_mixed):

    def group_step(operands):
        query_grp, key_grp, value_grp, log_grp, grad_grp = operands
        scores = (
            jnp.einsum("qhd,khd->hqk", query_grp, key_grp, preferred_element_type=jnp.float32)
            * 0.125
        )
        scores = jnp.where(allowed[None], scores, -1e30)
        soft_weights = jnp.exp(scores - log_grp[..., None])
        grad_soft = jnp.einsum(
            "qhd,khd->hqk", grad_grp, value_grp, preferred_element_type=jnp.float32
        )
        grad_value = jnp.einsum(
            "hqk,qhd->khd",
            soft_weights.astype(jnp.bfloat16),
            grad_grp,
            preferred_element_type=jnp.float32,
        )
        grad_scores = (
            soft_weights * (grad_soft - jnp.sum(soft_weights * grad_soft, axis=-1, keepdims=True))
        ).astype(jnp.bfloat16)
        grad_query = (
            jnp.einsum("hqk,khd->qhd", grad_scores, key_grp, preferred_element_type=jnp.float32)
            * 0.125
        )
        grad_key = (
            jnp.einsum("hqk,qhd->khd", grad_scores, query_grp, preferred_element_type=jnp.float32)
            * 0.125
        )
        return (grad_query, grad_key, grad_value)

    grad_query, grad_key, grad_value = lax.map(
        group_step,
        (
            split_heads(queries),
            split_heads(key_window),
            split_heads(value_window),
            log_total,
            split_heads(grad_mixed),
        ),
    )
    return (join_heads(grad_query), join_heads(grad_key), join_heads(grad_value))


def gather_forward(
    w_qkv,
    w_out,
    w_fc1,
    w_fc2,
    b_fc1,
    proj_bias,
    value_bias,
    ln_gain,
    ln_shift,
    layer_scale,
    layer_idx,
):
    return (
        lax.all_gather(w_qkv[layer_idx], "fsdp", axis=0, tiled=True),
        lax.all_gather(w_out[layer_idx], "fsdp", axis=0, tiled=True),
        lax.all_gather(w_fc1[layer_idx], "fsdp", axis=0, tiled=True),
        lax.all_gather(w_fc2[layer_idx], "fsdp", axis=0, tiled=True),
        lax.all_gather(b_fc1[layer_idx], "fsdp", axis=0, tiled=True),
        lax.all_gather(proj_bias[layer_idx], "fsdp", axis=1, tiled=True),
        lax.all_gather(value_bias[layer_idx], "fsdp", axis=0, tiled=True),
        lax.all_gather(ln_gain[layer_idx], "fsdp", axis=1, tiled=True),
        lax.all_gather(ln_shift[layer_idx], "fsdp", axis=1, tiled=True),
        lax.all_gather(layer_scale[layer_idx], "fsdp", axis=1, tiled=True),
    )


def gather_backward(
    w_qkv,
    w_out,
    w_fc1,
    w_fc2,
    b_fc1,
    proj_bias,
    value_bias,
    ln_gain,
    ln_shift,
    layer_scale,
    layer_idx,
):
    return (
        lax.all_gather(w_qkv[layer_idx], "fsdp", axis=0, tiled=True),
        lax.all_gather(w_out[layer_idx], "fsdp", axis=0, tiled=True),
        lax.all_gather(w_fc1[layer_idx], "fsdp", axis=0, tiled=True),
        lax.all_gather(w_fc2[layer_idx], "fsdp", axis=0, tiled=True),
        lax.all_gather(b_fc1[layer_idx], "fsdp", axis=0, tiled=True),
        lax.all_gather(proj_bias[layer_idx], "fsdp", axis=1, tiled=True),
        lax.all_gather(value_bias[layer_idx], "fsdp", axis=0, tiled=True),
        lax.all_gather(ln_gain[layer_idx], "fsdp", axis=1, tiled=True),
        lax.all_gather(ln_shift[layer_idx], "fsdp", axis=1, tiled=True),
        lax.all_gather(layer_scale[layer_idx], "fsdp", axis=1, tiled=True),
    )


def forward_layer(residual, weights, allowed):
    (
        qkv_weight,
        out_weight,
        fc1_weight,
        fc2_weight,
        fc1_bias,
        bias_rows,
        value_shift,
        gain_rows,
        shift_rows,
        scale_rows,
    ) = weights
    model_width = residual.shape[1]
    bias_f = bias_rows.astype(jnp.float32)
    gain_f = gain_rows.astype(jnp.float32)
    shift_f = shift_rows.astype(jnp.float32)
    scale_f = scale_rows.astype(jnp.float32)
    normed_in = layer_norm(residual, gain_f[0], shift_f[0]).astype(jnp.bfloat16)
    projected = jnp.dot(normed_in, qkv_weight, preferred_element_type=jnp.float32)
    queries = (projected[:, :model_width] + bias_f[0]).astype(jnp.bfloat16)
    key_rows = projected[:, model_width : 2 * model_width].astype(jnp.bfloat16)
    value_rows = (projected[:, 2 * model_width :] + value_shift.astype(jnp.float32)).astype(
        jnp.bfloat16
    )
    key_window, value_window = key_window_of(key_rows, value_rows)
    mixed_f, log_total = attend(queries, key_window, value_window, allowed)
    mixed = mixed_f.astype(jnp.bfloat16)
    branch_attn = jnp.dot(mixed, out_weight, preferred_element_type=jnp.float32) + bias_f[1]
    middle = residual + scale_f[0] * branch_attn
    normed_mid = layer_norm(middle, gain_f[1], shift_f[1]).astype(jnp.bfloat16)
    hidden = jnp.dot(normed_mid, fc1_weight, preferred_element_type=jnp.float32) + fc1_bias.astype(
        jnp.float32
    )
    active = gelu_exact(hidden).astype(jnp.bfloat16)
    branch_mlp = jnp.dot(active, fc2_weight, preferred_element_type=jnp.float32) + bias_f[2]
    result = middle + scale_f[1] * branch_mlp
    return (
        result,
        (
            residual,
            normed_in,
            queries,
            key_window,
            value_window,
            log_total,
            mixed,
            branch_attn,
            middle,
            normed_mid,
            hidden,
            active,
            branch_mlp,
        ),
    )


def backward_layer(grad_res, weights, kept_acts, allowed):
    (
        qkv_weight,
        out_weight,
        fc1_weight,
        fc2_weight,
        fc1_bias,
        bias_rows,
        value_shift,
        gain_rows,
        shift_rows,
        scale_rows,
    ) = weights
    (
        residual,
        normed_in,
        queries,
        key_window,
        value_window,
        log_total,
        mixed,
        branch_attn,
        middle,
        normed_mid,
        hidden,
        active,
        branch_mlp,
    ) = kept_acts
    row_count = residual.shape[0]
    model_width = residual.shape[1]
    gain_f = gain_rows.astype(jnp.float32)
    shift_f = shift_rows.astype(jnp.float32)
    scale_f = scale_rows.astype(jnp.float32)
    grad_scale_mlp = jnp.sum(grad_res * branch_mlp, axis=0)
    grad_branch_mlp = (scale_f[1] * grad_res).astype(jnp.bfloat16)
    grad_fc2 = contract_rows(active, grad_branch_mlp)
    grad_bias_mlp = jnp.sum(grad_branch_mlp.astype(jnp.float32), axis=0)
    grad_active = times_transposed(grad_branch_mlp, fc2_weight)
    gelu_out, gelu_pull = jax.vjp(gelu_exact, hidden)
    grad_hidden = gelu_pull(grad_active)[0].astype(jnp.bfloat16)
    grad_fc1 = contract_rows(normed_mid, grad_hidden)
    grad_fc1_bias = jnp.sum(grad_hidden.astype(jnp.float32), axis=0)
    grad_normed_mid = times_transposed(grad_hidden, fc1_weight)
    norm_out, norm_pull = jax.vjp(layer_norm, middle, gain_f[1], shift_f[1])
    grad_middle_part, grad_gain_mid, grad_shift_mid = norm_pull(grad_normed_mid)
    grad_middle = grad_res + grad_middle_part
    grad_scale_attn = jnp.sum(grad_middle * branch_attn, axis=0)
    grad_branch_attn = (scale_f[0] * grad_middle).astype(jnp.bfloat16)
    grad_out = contract_rows(mixed, grad_branch_attn)
    grad_bias_attn = jnp.sum(grad_branch_attn.astype(jnp.float32), axis=0)
    grad_mixed = times_transposed(grad_branch_attn, out_weight).astype(jnp.bfloat16)
    grad_queries, grad_key_window, grad_value_window = attend_back(
        queries, key_window, value_window, allowed, log_total, grad_mixed
    )
    grad_keys, grad_values = return_grads(grad_key_window, grad_value_window, row_count)
    grad_proj = jnp.concatenate(
        [
            grad_queries.astype(jnp.bfloat16),
            grad_keys.astype(jnp.bfloat16),
            grad_values.astype(jnp.bfloat16),
        ],
        axis=1,
    )
    grad_qkv = contract_rows(normed_in, grad_proj)
    grad_bias_query = jnp.sum(grad_proj[:, :model_width].astype(jnp.float32), axis=0)
    grad_value_shift = jnp.sum(grad_proj[:, 2 * model_width :].astype(jnp.float32), axis=0)
    grad_normed_in = times_transposed(grad_proj, qkv_weight)
    first_out, first_pull = jax.vjp(layer_norm, residual, gain_f[0], shift_f[0])
    grad_input_part, grad_gain_in, grad_shift_in = first_pull(grad_normed_in)
    grad_input = grad_middle + grad_input_part
    return (
        grad_input,
        (
            grad_qkv,
            grad_out,
            grad_fc1,
            grad_fc2,
            grad_fc1_bias,
            jnp.stack([grad_bias_query, grad_bias_attn, grad_bias_mlp]),
            grad_value_shift,
            jnp.stack([grad_gain_in, grad_gain_mid]),
            jnp.stack([grad_shift_in, grad_shift_mid]),
            jnp.stack([grad_scale_attn, grad_scale_mlp]),
        ),
    )


def local(
    tokens,
    image_ids,
    pad_mask,
    cotangent,
    w_qkv,
    w_out,
    w_fc1,
    w_fc2,
    b_fc1,
    proj_bias,
    value_bias,
    ln_gain,
    ln_shift,
    layer_scale,
):
    row_count = tokens.shape[0]
    window_ids, window_live = image_window(image_ids, pad_mask)
    columns = jnp.arange(window_ids.shape[0], dtype=jnp.int32)
    row_place = jnp.arange(row_count, dtype=jnp.int32)
    allowed = (image_ids[:, None] == window_ids[None, :]) & (window_live[None, :] == 1) | (
        columns[None, :] == row_place[:, None] + REACH * row_count
    )
    residual = tokens.astype(jnp.float32)
    saved_acts = []
    fetched = []
    for layer_idx in range(LAYERS):
        weights = gather_forward(
            w_qkv,
            w_out,
            w_fc1,
            w_fc2,
            b_fc1,
            proj_bias,
            value_bias,
            ln_gain,
            ln_shift,
            layer_scale,
            layer_idx,
        )
        fetched.append(weights)
        residual, kept_acts = forward_layer(residual, weights, allowed)
        saved_acts.append(kept_acts)
    output = residual.astype(jnp.bfloat16)
    grad_res = cotangent.astype(jnp.float32)
    shard_list = [None] * LAYERS
    for layer_idx in reversed(range(LAYERS)):
        weights = gather_backward(
            w_qkv,
            w_out,
            w_fc1,
            w_fc2,
            b_fc1,
            proj_bias,
            value_bias,
            ln_gain,
            ln_shift,
            layer_scale,
            layer_idx,
        )
        grad_res, gradients = backward_layer(grad_res, weights, saved_acts[layer_idx], allowed)
        (
            grad_qkv,
            grad_out,
            grad_fc1,
            grad_fc2,
            grad_fc1_bias,
            grad_bias_rows,
            grad_value_shift,
            grad_gain_rows,
            grad_shift_rows,
            grad_scale_rows,
        ) = gradients
        shard_sums = (
            lax.psum_scatter(
                grad_qkv.astype(jnp.bfloat16), "fsdp", scatter_dimension=0, tiled=True
            ).astype(jnp.float32),
            lax.psum_scatter(
                grad_out.astype(jnp.bfloat16), "fsdp", scatter_dimension=0, tiled=True
            ).astype(jnp.float32),
            lax.psum_scatter(
                grad_fc1.astype(jnp.bfloat16), "fsdp", scatter_dimension=0, tiled=True
            ).astype(jnp.float32),
            lax.psum_scatter(
                grad_fc2.astype(jnp.bfloat16), "fsdp", scatter_dimension=0, tiled=True
            ).astype(jnp.float32),
            lax.psum_scatter(
                grad_fc1_bias.astype(jnp.bfloat16), "fsdp", scatter_dimension=0, tiled=True
            ).astype(jnp.float32),
            lax.psum_scatter(
                grad_bias_rows.astype(jnp.bfloat16), "fsdp", scatter_dimension=1, tiled=True
            ).astype(jnp.float32),
            lax.psum_scatter(
                grad_value_shift.astype(jnp.bfloat16), "fsdp", scatter_dimension=0, tiled=True
            ).astype(jnp.float32),
            lax.psum_scatter(
                grad_gain_rows.astype(jnp.bfloat16), "fsdp", scatter_dimension=1, tiled=True
            ).astype(jnp.float32),
            lax.psum_scatter(
                grad_shift_rows.astype(jnp.bfloat16), "fsdp", scatter_dimension=1, tiled=True
            ).astype(jnp.float32),
            lax.psum_scatter(
                grad_scale_rows.astype(jnp.bfloat16), "fsdp", scatter_dimension=1, tiled=True
            ).astype(jnp.float32),
        )
        shard_sums = (
            lax.psum(shard_sums[0].astype(jnp.bfloat16), "dp").astype(jnp.float32),
            lax.psum(shard_sums[1].astype(jnp.bfloat16), "dp").astype(jnp.float32),
            lax.psum(shard_sums[2].astype(jnp.bfloat16), "dp").astype(jnp.float32),
            lax.psum(shard_sums[3].astype(jnp.bfloat16), "dp").astype(jnp.float32),
            lax.psum(shard_sums[4].astype(jnp.bfloat16), "dp").astype(jnp.float32),
            lax.psum(shard_sums[5].astype(jnp.bfloat16), "dp").astype(jnp.float32),
            lax.psum(shard_sums[6].astype(jnp.bfloat16), "dp").astype(jnp.float32),
            lax.psum(shard_sums[7].astype(jnp.bfloat16), "dp").astype(jnp.float32),
            lax.psum(shard_sums[8].astype(jnp.bfloat16), "dp").astype(jnp.float32),
            lax.psum(shard_sums[9].astype(jnp.bfloat16), "dp").astype(jnp.float32),
        )
        shard_list[layer_idx] = shard_sums
    stacked = [
        jnp.stack([shard_list[layer_idx][member] for layer_idx in range(LAYERS)])
        for member in range(10)
    ]
    return (
        output,
        grad_res.astype(jnp.bfloat16),
        stacked[0],
        stacked[1],
        stacked[2],
        stacked[3],
        stacked[4],
        stacked[5],
        stacked[6],
        stacked[7],
        stacked[8],
        stacked[9],
    )


def solution(mesh):
    in_specs = (
        P(("dp", "fsdp"), None),
        P(("dp", "fsdp")),
        P(("dp", "fsdp")),
        P(("dp", "fsdp"), None),
        P(None, "fsdp", None),
        P(None, "fsdp", None),
        P(None, "fsdp", None),
        P(None, "fsdp", None),
        P(None, "fsdp"),
        P(None, None, "fsdp"),
        P(None, "fsdp"),
        P(None, None, "fsdp"),
        P(None, None, "fsdp"),
        P(None, None, "fsdp"),
    )
    out_specs = (
        P(("dp", "fsdp"), None),
        P(("dp", "fsdp"), None),
        P(None, "fsdp", None),
        P(None, "fsdp", None),
        P(None, "fsdp", None),
        P(None, "fsdp", None),
        P(None, "fsdp"),
        P(None, None, "fsdp"),
        P(None, "fsdp"),
        P(None, None, "fsdp"),
        P(None, None, "fsdp"),
        P(None, None, "fsdp"),
    )
    return jax.shard_map(local, mesh=mesh, in_specs=in_specs, out_specs=out_specs, check_vma=False)
```

profile of v0, /device:TPU:0, one launch (start us, length us, event | category | flops | bytes accessed | tf_op | source)
XLA Modules:
  0.0 2958.1 jit_solution(6656872925481841520)
XLA Ops:
  127.6 24.6 collective-permute-done.17
  226.6 62.2 %collective-permute-done.5 = bf16[2,256,1024]{2,1,0:T(8,128)(2,1)} collective-permute-done((bf16[2,256,1024]{2,1,0:T(8,128)(2,1)}, bf16[2,256,1024]{2,1,0:T(8,128)(2,1)}, u32[]{:S(2)}, u32[]{:S(2)}) %collective-permute-start.5) | collective-permute-done | bytes 1048608 | tf_op jit(solution)/shard_map/ppermute | solution.py:14
  291.4 48.7 %collective-permute-done.6 = bf16[2,256,1024]{2,1,0:T(8,128)(2,1)} collective-permute-done((bf16[2,256,1024]{2,1,0:T(8,128)(2,1)}, bf16[2,256,1024]{2,1,0:T(8,128)(2,1)}, u32[]{:S(2)}, u32[]{:S(2)}) %collective-permute-start.6) | collective-permute-done | bytes 1048608 | tf_op jit(solution)/shard_map/ppermute | solution.py:14
  345.7 27.5 collective-permute-done.8
  399.4 104.6 %while.56 = (s32[]{:T(128)}, bf16[4,256,4,64]{1,3,2,0:T(8,128)(2,1)S(1)}, f32[4,4,256]{2,1,0:T(4,128)S(1)}, bf16[4,3328,4,64]{1,3,2,0:T(8,128)(2,1)}, bf16[4,256...) while((s32[]{:T(128)}, ...), condition=%wide.region_5.6_spmd.clone, body=%wide.region_2.5_spmd.clone.sunk | while | flops 916716544 | bytes 48157040 | solution.py:101
  533.1 33.7 %all-gather.37.cloned.1.call-done = bf16[1,1024,3072]{2,1,0:T(8,128)(2,1)} async-done(((bf16[1,512,3072]{2,1,0:T(8,128)(2,1)}), bf16[1,1024,3072]{2,1,0:T(8,128)(2,1)}) %all-gather.37.cloned.1.call-update) | async-done | bytes 6291472 | tf_op jit(solution)/shard_map/all_gather | solution.py:166
  623.2 93.3 %all-gather.18 = bf16[1,4096]{1,0:T(2,128)(2,1)S(1)} all-gather(bf16[1,2048]{1,0:T(2,128)(2,1)S(1)} %copy-done.93), channel_id=20, replica_groups=mesh['dp'=16,'fsdp'=2] {'fsdp'}, dimensions={1}, use_global_device_ids=true | all-gather | bytes 12288 | tf_op jit(solution)/shard_map/all_gather | solution.py:170
  748.9 38.7 %collective-permute-done.32 = bf16[2,256,1024]{2,1,0:T(8,128)(2,1)S(1)} collective-permute-done((bf16[2,256,1024]{2,1,0:T(8,128)(2,1)}, bf16[2,256,1024]{2,1,0:T(8,128)(2,1)S(1)}, u32[]{:S(2)}, u32[]{:S(2)}) %collective-permute-start.32) | collective-permute-done | bytes 1048608 | tf_op jit(solution)/shard_map/ppermute | solution.py:14
  787.6 35.1 %collective-permute-done.33 = bf16[2,256,1024]{2,1,0:T(8,128)(2,1)S(1)} collective-permute-done((bf16[2,256,1024]{2,1,0:T(8,128)(2,1)}, bf16[2,256,1024]{2,1,0:T(8,128)(2,1)S(1)}, u32[]{:S(2)}, u32[]{:S(2)}) %collective-permute-start.33) | collective-permute-done | bytes 1048608 | tf_op jit(solution)/shard_map/ppermute | solution.py:14
  854.6 103.3 %while.57 = (s32[]{:T(128)}, bf16[4,256,4,64]{1,3,2,0:T(8,128)(2,1)S(1)}, f32[4,4,256]{2,1,0:T(4,128)S(1)}, bf16[4,3328,4,64]{1,3,2,0:T(8,128)(2,1)}, bf16[4,256...) while((s32[]{:T(128)}, ...), condition=%wide.region_13.14_spmd.clone, body=%wide.region_10.13_spmd.clone.sunk | while | flops 916716544 | bytes 48157040 | solution.py:101
  1011.0 133.3 %while.58 = (s32[]{:T(128)}, bf16[4,256,4,64]{1,3,2,0:T(8,128)(2,1)}, f32[4,3328,4,64]{1,3,2,0:T(8,128)}, f32[4,3328,4,64]{1,3,2,0:T(8,128)}, bf16[4,3328,4,64]{...) while((s32[]{:T(128)}, ...), condition=%wide.region_20.21_spmd.clone, body=%wide.region_18.20_spmd.clone.sunk | while | flops 2216033280 | bytes 148155872 | solution.py:139
  1196.1 31.4 %collective-permute-done.38 = bf16[2,256,1024]{1,2,0:T(8,128)(2,1)S(1)} collective-permute-done((bf16[2,256,1024]{1,2,0:T(8,128)(2,1)S(1)}, bf16[2,256,1024]{1,2,0:T(8,128)(2,1)S(1)}, u32[]{:S(2)}, u32[]{:S(2)}) %collective-permute-start.38) | collective-permute-done | bytes 1048608 | tf_op jit(solution)/shard_map/ppermute | solution.py:14
  1269.0 34.6 %collective-permute-start.45 = (bf16[2,256,1024]{1,2,0:T(8,128)(2,1)}, bf16[2,256,1024]{1,2,0:T(8,128)(2,1)}, u32[]{:S(2)}, u32[]{:S(2)}) collective-permute-start(bf16[2,256,1024]{1,2,0:T(8,128)(2,1)} %get-tuple-element.526), channel_id=1, source_target_pairs={{0,4},{1,5},{2,6},{3,7},{4,8},{5,9},{6,10},{7,11},{8,12},{9,13},{1... | collective-permute-start | bytes 3145736 | tf_op jit(solution)/shard_map/ppermute | solution.py:14
  1327.1 25.7 collective-permute-done.45
  1352.8 22.3 collective-permute-done.47
  1445.7 137.2 %while.59 = (s32[]{:T(128)}, bf16[4,256,4,64]{1,3,2,0:T(8,128)(2,1)}, f32[4,3328,4,64]{1,3,2,0:T(8,128)}, f32[4,3328,4,64]{1,3,2,0:T(8,128)}, bf16[4,3328,4,64]{...) while((s32[]{:T(128)}, ...), condition=%wide.region_27.28_spmd.clone, body=%wide.region_25.27_spmd.clone.sunk | while | flops 2216033280 | bytes 148155872 | solution.py:139
  1618.7 66.4 %collective-permute-done.48 = bf16[2,256,1024]{1,2,0:T(8,128)(2,1)S(1)} collective-permute-done((bf16[2,256,1024]{1,2,0:T(8,128)(2,1)}, bf16[2,256,1024]{1,2,0:T(8,128)(2,1)S(1)}, u32[]{:S(2)}, u32[]{:S(2)}) %collective-permute-start.48) | collective-permute-done | bytes 1048608 | tf_op jit(solution)/shard_map/ppermute | solution.py:14
  1872.3 84.8 %reduce-scatter.33.cloned.1.call-done = bf16[512,3072]{1,0:T(8,128)(2,1)} async-done(((bf16[1024,3072]{1,0:T(8,128)(2,1)}), bf16[512,3072]{1,0:T(8,128)(2,1)}) %reduce-scatter.33.cloned.1.call-update) | async-done | bytes 3145744 | tf_op jit(solution)/shard_map/reduce_scatter | solution.py:424
  1957.1 102.2 %reduce-scatter.43.cloned.1.call-done = bf16[512,4096]{1,0:T(8,128)(2,1)} async-done(((bf16[1024,4096]{1,0:T(8,128)(2,1)}), bf16[512,4096]{1,0:T(8,128)(2,1)}) %reduce-scatter.43.cloned.1.call-update) | async-done | bytes 4194320 | tf_op jit(solution)/shard_map/reduce_scatter | solution.py:430
  2059.4 102.1 %reduce-scatter.47.cloned.1.call-done = bf16[2048,1024]{1,0:T(8,128)(2,1)} async-done(((bf16[4096,1024]{1,0:T(8,128)(2,1)}), bf16[2048,1024]{1,0:T(8,128)(2,1)}) %reduce-scatter.47.cloned.1.call-update) | async-done | bytes 4194320 | tf_op jit(solution)/shard_map/reduce_scatter | solution.py:433
  2161.5 101.5 %reduce-scatter.45.cloned.1.call-done = bf16[2048,1024]{1,0:T(8,128)(2,1)} async-done(((bf16[4096,1024]{1,0:T(8,128)(2,1)}), bf16[2048,1024]{1,0:T(8,128)(2,1)}) %reduce-scatter.45.cloned.1.call-update) | async-done | bytes 4194320 | tf_op jit(solution)/shard_map/reduce_scatter | solution.py:433
  2263.0 102.1 %reduce-scatter.41.cloned.1.call-done = bf16[512,4096]{1,0:T(8,128)(2,1)} async-done(((bf16[1024,4096]{1,0:T(8,128)(2,1)}), bf16[512,4096]{1,0:T(8,128)(2,1)}) %reduce-scatter.41.cloned.1.call-update) | async-done | bytes 4194320 | tf_op jit(solution)/shard_map/reduce_scatter | solution.py:430
  2478.3 64.6 %all-reduce.4 = (bf16[1,2048]{1,0:T(2,128)(2,1)S(1)}, bf16[1,2048]{1,0:T(2,128)(2,1)S(1)}, bf16[1,3,512]{2,1,0:T(4,128)(2,1)S(1)}, bf16[1,3,512]{2,1,0:T(4,128)(...) all-reduce(bf16[1,2048]{1,0:T(2,128)(2,1)S(1)} %stack.289, ...), channel_id=1, replica_groups=mesh['dp'=16,'fsdp'=2] {'dp'}, use_global_device_ids=true, to_apply=%region_51.52 | all-reduce | flops 14336 | bytes 57344 | tf_op jit(solution)/shard_map/psum | solution.py:460
  2546.0 374.7 %all-reduce.9.cloned.1.call-done = (bf16[1,512,3072]{2,1,0:T(8,128)(2,1)}, bf16[1,512,3072]{2,1,0:T(8,128)(2,1)}, bf16[1,512,1024]{2,1,0:T(8,128)(2,1)}, bf16[1,...) async-done(((bf16[1,512,3072]{2,1,0:T(8,128)(2,1)}, ...) | async-done | bytes 25165840 | tf_op jit(solution)/shard_map/psum | solution.py:456
  (877 shorter events, 1462.3 us)
Async XLA Ops:
  13.2 490.9 %all-gather.31.cloned.1.call-start = ((), (), s32[]{:S(2)}) async-start(), calls=%async_computation.25 | async-start | bytes 3145728 | tf_op jit(solution)/shard_map/all_gather | solution.py:167
  16.3 491.9 %all-gather.33.cloned.1.call-start = ((), (), s32[]{:S(2)}) async-start(), calls=%async_computation.26 | async-start | bytes 12582912 | tf_op jit(solution)/shard_map/all_gather | solution.py:168
  22.4 502.9 %all-gather.35.cloned.1.call-start = ((), (), s32[]{:S(2)}) async-start(), calls=%async_computation.27 | async-start | bytes 12582912 | tf_op jit(solution)/shard_map/all_gather | solution.py:169
  30.5 536.3 %all-gather.37.cloned.1.call-start = ((), (), s32[]{:S(2)}) async-start(), calls=%async_computation.28 | async-start | bytes 9437184 | tf_op jit(solution)/shard_map/all_gather | solution.py:166
  31.1 926.8 %all-gather.39.cloned.1.call-start = ((), (), s32[]{:S(2)}) async-start(), calls=%async_computation.29 | async-start | bytes 3145728 | tf_op jit(solution)/shard_map/all_gather | solution.py:167
  31.7 930.0 %all-gather.41.cloned.1.call-start = ((), (), s32[]{:S(2)}) async-start(), calls=%async_computation.30 | async-start | bytes 12582912 | tf_op jit(solution)/shard_map/all_gather | solution.py:168
  45.5 932.8 %all-gather.43.cloned.1.call-start = ((), (), s32[]{:S(2)}) async-start(), calls=%async_computation.31 | async-start | bytes 12582912 | tf_op jit(solution)/shard_map/all_gather | solution.py:169
  623.2 1249.1 %reduce-scatter.39.cloned.1.call-start = ((), (), s32[]{:S(2)}) async-start(), calls=%async_computation.19 | async-start | bytes 3145728 | tf_op jit(solution)/shard_map/reduce_scatter | solution.py:427
  1327.0 545.3 %reduce-scatter.37.cloned.1.call-start = ((), (), s32[]{:S(2)}) async-start(), calls=%async_computation.18 | async-start | bytes 3145728 | tf_op jit(solution)/shard_map/reduce_scatter | solution.py:427
  1422.4 449.9 %reduce-scatter.35.cloned.1.call-start = ((), (), s32[]{:S(2)}) async-start(), calls=%async_computation.17 | async-start | bytes 9437184 | tf_op jit(solution)/shard_map/reduce_scatter | solution.py:424
  1431.7 525.5 %reduce-scatter.33.cloned.1.call-start = ((), (), s32[]{:S(2)}) async-start(), calls=%async_computation.16 | async-start | bytes 9437184 | tf_op jit(solution)/shard_map/reduce_scatter | solution.py:424
  1822.7 236.6 %reduce-scatter.43.cloned.1.call-start = ((), (), s32[]{:S(2)}) async-start(), calls=%async_computation.21 | async-start | bytes 12582912 | tf_op jit(solution)/shard_map/reduce_scatter | solution.py:430
  1831.4 330.0 %reduce-scatter.47.cloned.1.call-start = ((), (), s32[]{:S(2)}) async-start(), calls=%async_computation.23 | async-start | bytes 12582912 | tf_op jit(solution)/shard_map/reduce_scatter | solution.py:433
  1839.9 423.1 %reduce-scatter.45.cloned.1.call-start = ((), (), s32[]{:S(2)}) async-start(), calls=%async_computation.22 | async-start | bytes 12582912 | tf_op jit(solution)/shard_map/reduce_scatter | solution.py:433
  1848.3 516.8 %reduce-scatter.41.cloned.1.call-start = ((), (), s32[]{:S(2)}) async-start(), calls=%async_computation.20 | async-start | bytes 12582912 | tf_op jit(solution)/shard_map/reduce_scatter | solution.py:430
  1857.1 522.4 %reduce-scatter.51.cloned.1.call-start = ((), (), s32[]{:S(2)}) async-start(), calls=%async_computation.33 | async-start | bytes 393216
  1859.3 534.1 %reduce-scatter.61.cloned.1.call-start = ((), (), s32[]{:S(2)}) async-start(), calls=%async_computation.38 | async-start | bytes 393216
  1860.4 547.1 %reduce-scatter.63.cloned.1.call-start = ((), (), s32[]{:S(2)}) async-start(), calls=%async_computation.39 | async-start | bytes 393216
  1861.3 559.9 %reduce-scatter.59.cloned.1.call-start = ((), (), s32[]{:S(2)}) async-start(), calls=%async_computation.37 | async-start | bytes 393216
  1862.3 573.0 %reduce-scatter.55.cloned.1.call-start = ((), (), s32[]{:S(2)}) async-start(), calls=%async_computation.35 | async-start | bytes 393216
  1863.7 585.7 %reduce-scatter.49.cloned.1.call-start = ((), (), s32[]{:S(2)}) async-start(), calls=%async_computation.32 | async-start | bytes 393216
  1864.7 598.7 %reduce-scatter.57.cloned.1.call-start = ((), (), s32[]{:S(2)}) async-start(), calls=%async_computation.36 | async-start | bytes 393216
  1871.2 606.0 %reduce-scatter.53.cloned.1.call-start = ((), (), s32[]{:S(2)}) async-start(), calls=%async_computation.34 | async-start | bytes 393216
  1872.2 1048.5 %all-reduce.9.cloned.1.call-start = ((), (), s32[]{:S(2)}) async-start(), calls=%async_computation.40 | async-start | bytes 50331648 | tf_op jit(solution)/shard_map/psum | solution.py:456
  (244 other events, 10420.0 us)
Sparse Core Ops, SparseCore 0:
  13.4 83.6 all-gather.28
  98.6 41.1 all-gather.30
  142.0 231.4 all-gather.32
  374.8 110.2 all-gather.34
  486.5 80.3 all-gather.36
  568.2 49.8 all-gather.38
  620.2 181.2 all-gather.40
  803.1 128.6 all-gather.42
  1327.1 53.8 reduce-scatter.38
  1422.5 59.3 reduce-scatter.36
  1484.2 77.1 reduce-scatter.34
  1822.8 134.2 reduce-scatter.32
  1960.0 99.3 reduce-scatter.42
  2062.1 99.3 reduce-scatter.46
  2163.6 99.3 reduce-scatter.44
  2265.7 99.3 reduce-scatter.40
  2367.7 11.7 reduce-scatter.50
  2381.6 11.7 reduce-scatter.60
  2395.6 11.7 reduce-scatter.62
  2409.5 11.7 reduce-scatter.58
  2423.5 11.7 reduce-scatter.54
  2437.6 11.7 reduce-scatter.48
  2451.6 11.7 reduce-scatter.56
  2483.0 437.6 all-reduce.8
  (1 shorter events, 11.7 us)
where the time goes:
time: 2970 us; the launch traced here: 2960 us
  waiting for transfers between devices  1550 us (52%)
  matrix products  488 us (16%)
  starting transfers between devices  283 us (10%)
  other arithmetic  222 us (7%)
  blocking collectives  216 us (7%)
  local copies, waits for them, and re-layouts  180 us (6%)
    ppermute x60, waiting for transfers between devices, passed_along(): return lax.ppermute(x, axis, pairs)  545 us
    psum x1, waiting for transfers between devices, local(): lax.psum(shard_sums[0].astype(jnp.bfloat16), 'dp').astype(jnp.float32)  375 us
    ppermute x60, starting transfers between devices, passed_along(): return lax.ppermute(x, axis, pairs)  281 us
    reduce_scatter x2, waiting for transfers between devices, local(): lax.psum_scatter(grad_fc1.astype(jnp.bfloat16), 'fsdp', scatter_dimension...  204 us
    reduce_scatter x2, waiting for transfers between devices, local(): lax.psum_scatter(grad_fc2.astype(jnp.bfloat16), 'fsdp', scatter_dimension...  204 us
    dot_general x16, matrix products, group_step(): jnp.einsum('qhd,khd->hqk', query_grp, key_grp, preferred_element_type=jnp...  132 us
    all_gather x2, blocking collectives, gather_forward(): lax.all_gather(b_fc1[layer_idx], 'fsdp', axis=0, tiled=True)  97.8 us
    unnamed x33, waiting for transfers between devices  95.5 us
  transfers between devices with their start and end apart: 85, of which 40 were waited for; matrix products, arithmetic and copies ran while one was open for 22% of the time, Pallas kernels for 0%

commit v1 on v0

v1 whole, which is shorter than its diff:
```python
import jax
import jax.numpy as jnp
from jax import lax
from jax.experimental import pallas as pl
from jax.experimental.pallas import tpu as pltpu
from jax.sharding import Mesh
from jax.sharding import PartitionSpec as P


HD = 64
LAYERS = 2
REACH = 6
GROUP = 8
LANES = 128
KEYS = 1536
KEYS_BACK = 768
BF = jnp.bfloat16
F32 = jnp.float32
ALL = ("z", "y", "c", "x")

QKV, OUT, FC1, FC2 = range(4)
UNITS = ((QKV, 0, 3), (QKV, 0, 1), (QKV, 1, 2), (OUT, 0, 1), (FC1, 0, 2), (FC1, 2, 2), (FC2, 0, 2), (FC2, 2, 2))
NQKV, NQ, NKV, NOUT, FC1A, FC1B, FC2A, FC2B = range(8)
GROUPS = ((NOUT, NQKV), (FC1A, FC1B), (FC2A, FC2B), (NOUT, NQ), (NKV,))
GQ, G1, G2, GA, GB = range(5)
USED = ((G2, G1, GA, GB), (G2, G1, GQ))
BY_HAND = ((G2, 0), (GA, 0), (GB, 0))


DP = ("z", "y", "c")


def layer_norm(values, gain_row, shift_row):
    centre = values - jnp.mean(values, axis=-1, keepdims=True)
    spread = jnp.mean(centre * centre, axis=-1, keepdims=True)
    return centre * lax.rsqrt(spread + 1e-06) * gain_row + shift_row


def nn(a, b):
    return lax.dot_general(a, b, (((1,), (0,)), ((), ())), preferred_element_type=F32)


def nt(a, b):
    return lax.dot_general(a, b, (((1,), (1,)), ((), ())), preferred_element_type=F32)


def tn(a, b):
    return lax.dot_general(a, b, (((0,), (0,)), ((), ())), preferred_element_type=F32)


def masked_heads(value, low):
    return jnp.concatenate([jnp.where(low, value, 0.0), jnp.where(low, 0.0, value)], axis=0).astype(BF)


def key_range(lo_ref, hi_ref, blocks, chunk):
    i = pl.program_id(0)
    trips = (hi_ref[i] - lo_ref[i] + chunk - 1) // chunk
    return jnp.minimum(lo_ref[i], blocks - trips * chunk), trips


def attn_fwd_kernel(lo_ref, hi_ref, q_ref, k_ref, v_ref, qid_ref, kid_ref, o_ref, of_ref, lse_ref, s_scr, m_scr, l_scr, a_scr):
    blk = q_ref.shape[0]
    span = s_scr.shape[2]
    chunk = span // LANES
    low = lax.broadcasted_iota(jnp.int32, (blk, 2 * HD), 1) < HD
    q2 = masked_heads(q_ref[...].astype(F32) * 0.125, low)
    qid = qid_ref[...]
    qid2 = jnp.broadcast_to(jnp.concatenate([qid, qid], axis=0), (2 * blk, LANES))
    lo, trips = key_range(lo_ref, hi_ref, kid_ref.shape[0], chunk)
    m_scr[...] = jnp.full_like(m_scr, -1e30)
    l_scr[...] = jnp.zeros_like(l_scr)
    a_scr[...] = jnp.zeros_like(a_scr)

    def scores(t, carry):
        at = lo + t * chunk
        s = nt(q2, k_ref[pl.ds(pl.multiple_of(at * LANES, LANES), span), :])
        top = m_scr[...]
        for part in range(chunk):
            cols = slice(part * LANES, (part + 1) * LANES)
            piece = jnp.where(qid2 == kid_ref[at + part], s[:, cols], -1e30)
            s_scr[t, :, cols] = piece
            top = jnp.maximum(top, piece)
        m_scr[...] = top
        return carry

    lax.fori_loop(0, trips, scores, 0)
    row_top = jnp.max(m_scr[...], axis=1, keepdims=True)
    top = jnp.broadcast_to(row_top, (2 * blk, LANES))

    def mix(t, carry):
        v = v_ref[pl.ds(pl.multiple_of((lo + t * chunk) * LANES, LANES), span), :]
        total = l_scr[...]
        probs = []
        for part in range(chunk):
            p = jnp.exp(s_scr[t, :, part * LANES : (part + 1) * LANES] - top)
            total = total + p
            probs.append(p.astype(BF))
        l_scr[...] = total
        a_scr[...] += nn(jnp.concatenate(probs, axis=1), v)
        return carry

    lax.fori_loop(0, trips, mix, 0)
    row_total = jnp.sum(l_scr[...], axis=1, keepdims=True)
    out = a_scr[...] / row_total
    mixed = jnp.where(low, out[:blk], out[blk:])
    o_ref[...] = mixed.astype(BF)
    of_ref[...] = mixed
    lse = jnp.broadcast_to(row_top + jnp.log(row_total), (2 * blk, LANES))
    lse_ref[0] = jnp.transpose(lse)[0:1, :]


def attn_fwd(qkv, kv_win, qid_col, kid_row, lo, hi):
    rows = qkv.shape[0]
    blk = rows // lo.shape[0]
    span = kv_win.shape[0]
    wide = 2 * HD
    most = -(-((2 * REACH + 1) * blk + LANES) // KEYS)
    pairs = rows * blk * 7 * 2
    return pl.pallas_call(
        attn_fwd_kernel,
        grid_spec=pltpu.PrefetchScalarGridSpec(
            num_scalar_prefetch=2,
            grid=(rows // blk,),
            in_specs=[
                pl.BlockSpec((blk, wide), lambda i, lo, hi: (i, 0)),
                pl.BlockSpec((span, wide), lambda i, lo, hi: (0, 0)),
                pl.BlockSpec((span, wide), lambda i, lo, hi: (0, 1)),
                pl.BlockSpec((blk, 1), lambda i, lo, hi: (i, 0)),
                pl.BlockSpec(kid_row.shape, lambda i, lo, hi: (0, 0, 0)),
            ],
            out_specs=[
                pl.BlockSpec((blk, wide), lambda i, lo, hi: (i, 0)),
                pl.BlockSpec((blk, wide), lambda i, lo, hi: (i, 0)),
                pl.BlockSpec((1, 1, 2 * blk), lambda i, lo, hi: (i, 0, 0)),
            ],
            scratch_shapes=[pltpu.VMEM((most, 2 * blk, KEYS), F32)] + [pltpu.VMEM((2 * blk, LANES), F32)] * 3,
        ),
        out_shape=[
            jax.ShapeDtypeStruct((rows, wide), BF),
            jax.ShapeDtypeStruct((rows, wide), F32),
            jax.ShapeDtypeStruct((rows // blk, 1, 2 * blk), F32),
        ],
        cost_estimate=pl.CostEstimate(
            flops=pairs * wide * 4, bytes_accessed=span * wide * 4 + rows * wide * 8, transcendentals=pairs
        ),
        name="attn_fwd",
    )(lo, hi, qkv, kv_win, kv_win, qid_col, kid_row)


def attn_bwd_kernel(
    lo_ref, hi_ref, q_ref, k_ref, v_ref, do_ref, qid_ref, kid_ref, lse_ref, of_ref, dq_ref, own_ref, prev_ref, next_ref, dk_scr, dv_scr, dq_scr
):
    blk = q_ref.shape[0]
    i = pl.program_id(0)
    halo = prev_ref.shape[0]
    rows = own_ref.shape[0]
    wide = 2 * HD
    low = lax.broadcasted_iota(jnp.int32, (blk, wide), 1) < HD

    @pl.when(i == 0)
    def _():
        dk_scr[...] = jnp.zeros_like(dk_scr)
        dv_scr[...] = jnp.zeros_like(dv_scr)

    q2 = masked_heads(q_ref[...].astype(F32) * 0.125, low)
    grad = do_ref[...].astype(F32)
    g2 = masked_heads(grad, low)
    picks = jnp.where(lax.broadcasted_iota(jnp.int32, (8, wide), 1) < HD, 1.0, 0.0)
    dots = [
        lax.dot_general(
            pick, grad * of_ref[...], (((1,), (1,)), ((), ())), precision=lax.Precision.HIGHEST, preferred_element_type=F32
        )
        for pick in (picks, 1.0 - picks)
    ]
    dd = jnp.concatenate([d[0:1] for d in dots], axis=1)
    qid = qid_ref[0]
    lse = lse_ref[0]
    chunk = KEYS_BACK // LANES
    lo, trips = key_range(lo_ref, hi_ref, k_ref.shape[0] // LANES, chunk)
    dq_scr[...] = jnp.zeros_like(dq_scr)

    def step(t, carry):
        at = pl.ds(pl.multiple_of((lo + t * chunk) * LANES, LANES), KEYS_BACK)
        k = k_ref[at, :]
        v = v_ref[at, :]
        s = nt(k, q2)
        p = jnp.where(kid_ref[at, :] == qid, jnp.exp(s - lse), 0.0)
        dp = nt(v, g2)
        ds = (p * (dp - dd)).astype(BF)
        dv_scr[at, :] += nn(p.astype(BF), g2)
        dk_scr[at, :] += nn(ds, q2)
        dq_scr[...] += tn(ds, k)
        return carry

    lax.fori_loop(0, trips, step, 0)
    dq = dq_scr[...]
    dq_ref[...] = (jnp.where(low, dq[:blk], dq[blk:]) * 0.125).astype(BF)

    @pl.when(i == pl.num_programs(0) - 1)
    def _():
        for side, scr in enumerate((dk_scr, dv_scr)):
            cols = pl.ds(side * wide, wide)
            prev_ref[:, cols] = scr[pl.ds(0, halo), :].astype(BF)
            own_ref[:, cols] = scr[pl.ds(halo, rows), :]
            next_ref[:, cols] = scr[pl.ds(halo + rows, halo), :].astype(BF)


def attn_bwd(qkv, kv_win, grad_out, qid_row, kid_col, lse, mixed, lo, hi):
    rows = qkv.shape[0]
    blk = rows // qid_row.shape[0]
    span = kv_win.shape[0]
    halo = (span - rows) // 2
    wide = 2 * HD
    pairs = rows * blk * 7 * 2
    row_spec = pl.BlockSpec((1, 1, 2 * blk), lambda i, lo, hi: (i, 0, 0))
    return pl.pallas_call(
        attn_bwd_kernel,
        grid_spec=pltpu.PrefetchScalarGridSpec(
            num_scalar_prefetch=2,
            grid=(rows // blk,),
            in_specs=[
                pl.BlockSpec((blk, wide), lambda i, lo, hi: (i, 0)),
                pl.BlockSpec((span, wide), lambda i, lo, hi: (0, 0)),
                pl.BlockSpec((span, wide), lambda i, lo, hi: (0, 1)),
                pl.BlockSpec((blk, wide), lambda i, lo, hi: (i, 0)),
                row_spec,
                pl.BlockSpec((span, 1), lambda i, lo, hi: (0, 0)),
                row_spec,
                pl.BlockSpec((blk, wide), lambda i, lo, hi: (i, 0)),
            ],
            out_specs=[
                pl.BlockSpec((blk, wide), lambda i, lo, hi: (i, 0)),
                pl.BlockSpec((rows, 2 * wide), lambda i, lo, hi: (0, 0)),
                pl.BlockSpec((halo, 2 * wide), lambda i, lo, hi: (0, 0)),
                pl.BlockSpec((halo, 2 * wide), lambda i, lo, hi: (0, 0)),
            ],
            scratch_shapes=[pltpu.VMEM((span, wide), F32)] * 2 + [pltpu.VMEM((2 * blk, wide), F32)],
        ),
        out_shape=[
            jax.ShapeDtypeStruct((rows, wide), BF),
            jax.ShapeDtypeStruct((rows, 2 * wide), F32),
            jax.ShapeDtypeStruct((halo, 2 * wide), BF),
            jax.ShapeDtypeStruct((halo, 2 * wide), BF),
        ],
        cost_estimate=pl.CostEstimate(
            flops=pairs * wide * 10, bytes_accessed=span * wide * 12 + rows * wide * 12, transcendentals=pairs
        ),
        name="attn_bwd",
    )(lo, hi, qkv, kv_win, kv_win, grad_out, qid_row, kid_col, lse, mixed)


def lanes(start, size):
    return pl.ds(pl.multiple_of(start, 128), size)


def gelu_parts(values):
    share = 0.5 * (1.0 + lax.erf(values * 0.7071067811865476))
    slope = share + values * (0.3989422804014327 * jnp.exp(-0.5 * values * values))
    return values * share, slope


def halves_sum(start_ref, acts_ref, own_ref, other_refs):
    total = nn(acts_ref[:, lanes(start_ref[0], own_ref.shape[1])], own_ref[0])
    for k, ref in enumerate(other_refs):
        total += nn(acts_ref[:, lanes(start_ref[k + 1], ref.shape[0])], ref[...])
    return total


def qkv_kernel(start_ref, acts_ref, own_ref, *refs):
    others, bias_ref, out_ref = refs[:-2], refs[-2], refs[-1]
    proj = halves_sum(start_ref, acts_ref, own_ref, others) + bias_ref[0]
    wide = out_ref.shape[2]
    for g in range(GROUP):
        out_ref[g] = proj[:, g * wide : (g + 1) * wide].astype(BF)


def fc1_kernel(start_ref, acts_ref, own_ref, *refs):
    others, bias_ref, active_ref, slope_ref = refs[:-3], *refs[-3:]
    value, slope = gelu_parts(halves_sum(start_ref, acts_ref, own_ref, others) + bias_ref[0])
    active_ref[...] = value.astype(BF)
    slope_ref[...] = slope.astype(BF)


def plain_kernel(start_ref, acts_ref, own_ref, *refs):
    others, bias_ref, out_ref = refs[:-2], refs[-2], refs[-1]
    out_ref[...] = halves_sum(start_ref, acts_ref, own_ref, others) + bias_ref[0]


def other_spec(tall, wide, at):
    first = at // wide
    return pl.BlockSpec((tall, wide), lambda j, start: (0, first + j))


def product(kernel, acts, own, layer, others, starts, wide, bias, out_specs, out_shape):
    tokens = acts.shape[0]
    tall, width = own.shape[1:]
    steps = width // wide
    return pl.pallas_call(
        kernel,
        grid_spec=pltpu.PrefetchScalarGridSpec(
            num_scalar_prefetch=1,
            grid=(steps,),
            in_specs=[
                pl.BlockSpec(acts.shape, lambda j, start: (0, 0)),
                pl.BlockSpec((1, tall, wide), lambda j, start: (layer, 0, j)),
                *[other_spec(rows, wide, at) for _, rows, at in others],
                pl.BlockSpec((1, 1, wide), lambda j, start: (j, 0, 0)),
            ],
            out_specs=out_specs,
        ),
        out_shape=out_shape,
        cost_estimate=pl.CostEstimate(
            flops=4 * tokens * tall * width, bytes_accessed=4 * tall * width + 6 * tokens * width, transcendentals=0
        ),
    )(starts, acts, own, *[array for array, _, _ in others], bias.reshape(steps, 1, wide))


def gact_kernel(start_ref, grad_ref, own_ref, *refs):
    others, slope_ref, out_ref, sum_ref = refs[:-3], *refs[-3:]
    weights = [own_ref[0]] + [ref[...] for ref in others]
    for n, weight in enumerate(weights):
        at = lanes(start_ref[n] + pl.program_id(0) * weight.shape[0], weight.shape[0])
        grad = (nt(grad_ref[...], weight) * slope_ref[:, at].astype(F32)).astype(BF)
        out_ref[:, at] = grad
        sum_ref[:, at] = jnp.sum(grad.astype(F32), axis=0, keepdims=True)


def dx_kernel(start_ref, grad_ref, own_ref, other_refs, out_ref):
    weights = [own_ref[0]] + [ref[...] for ref in other_refs]
    for n, weight in enumerate(weights):
        at = lanes(start_ref[n], weight.shape[0])
        term = nt(grad_ref[...], weight)

        @pl.when(pl.program_id(0) == 0)
        def _():
            out_ref[:, at] = term

        @pl.when(pl.program_id(0) > 0)
        def _():
            out_ref[:, at] += term


def dx_plain_kernel(start_ref, grad_ref, own_ref, *refs):
    dx_kernel(start_ref, grad_ref, own_ref, refs[:-1], refs[-1])


def dx_qkv_kernel(start_ref, heads_ref, own_ref, *refs):
    others, out_ref, grad_ref = refs[:-2], refs[-2], refs[-1]
    wide = heads_ref.shape[2]
    for g in range(GROUP):
        grad_ref[:, g * wide : (g + 1) * wide] = heads_ref[g]
    dx_kernel(start_ref, grad_ref, own_ref, others, out_ref)


def dx_out_kernel(start_ref, grad_ref, own_ref, *refs):
    others, out_ref, scr = refs[:-2], refs[-2], refs[-1]
    dx_kernel(start_ref, grad_ref, own_ref, others, scr)
    wide = out_ref.shape[2]

    @pl.when(pl.program_id(0) == pl.num_programs(0) - 1)
    def _():
        for g in range(GROUP):
            out_ref[g] = scr[:, g * wide : (g + 1) * wide].astype(BF)


def product_back(kernel, grad, grad_spec, own, layer, others, starts, wide, out_specs, out_shape, scratch=()):
    tall, width = own.shape[1:]
    return pl.pallas_call(
        kernel,
        grid_spec=pltpu.PrefetchScalarGridSpec(
            num_scalar_prefetch=1,
            grid=(width // wide,),
            in_specs=[
                grad_spec,
                pl.BlockSpec((1, tall, wide), lambda j, start: (layer, 0, j)),
                *[other_spec(rows, wide, at) for _, rows, at in others],
            ],
            out_specs=out_specs,
            scratch_shapes=list(scratch),
        ),
        out_shape=out_shape,
        cost_estimate=pl.CostEstimate(
            flops=1024 * tall * width, bytes_accessed=4 * tall * width + 1024 * (tall + width), transcendentals=0
        ),
    )(starts, grad, own, *[array for array, _, _ in others])


QUARTER = 256
WIDE = 1024


def split_rows(scr, side, keep_ref, away_ref):
    half = keep_ref.shape[0]
    keep_ref[...] = scr[pl.ds(pl.multiple_of(side * half, half), half), :].astype(BF)
    away_ref[...] = scr[pl.ds(pl.multiple_of((1 - side) * half, half), half), :].astype(BF)


def away_kernel(spot_ref, mine_ref, theirs_ref, cols_ref, cols2_ref, out_ref):
    out_ref[...] = (tn(mine_ref[...], cols_ref[...]) + tn(theirs_ref[...], cols2_ref[...])).astype(BF)


def keep_kernel(spot_ref, mine_ref, theirs_ref, cols_ref, cols2_ref, came_ref, *refs):
    keep_ref, away_ref, scr = refs[-3:]
    scr[...] = tn(mine_ref[...], cols_ref[...]) + tn(theirs_ref[...], cols2_ref[...]) + came_ref[...].astype(F32)
    split_rows(scr, spot_ref[2], keep_ref, away_ref)


def block_grad(mine, theirs, cols, cols2, spot, first, steps, came=None, into=None, at=0, whole=0):
    tokens, depth = mine.shape
    width = cols.shape[1]
    subs = depth // (4 * QUARTER)
    over = (lambda j: 0) if subs > 1 else (lambda j: first + j)
    sub = (lambda j: first + j) if subs > 1 else (lambda j: 0)
    col = pl.BlockSpec((tokens, WIDE), lambda j, spot: (0, over(j)))
    in_specs = [
        pl.BlockSpec((tokens, QUARTER), lambda j, spot: (0, (spot[0] * 2 + spot[1]) * subs + sub(j))),
        pl.BlockSpec((tokens, QUARTER), lambda j, spot: (0, spot[0] * subs + sub(j))),
        col,
        col,
    ]
    operands = [mine, theirs, cols, cols2]
    scratch = []
    aliases = {}
    if came is None:
        kernel = away_kernel
        out_specs = pl.BlockSpec((QUARTER, WIDE), lambda j, spot: (0, j))
        out_shape = jax.ShapeDtypeStruct((QUARTER, steps * WIDE), BF)
    else:
        kernel = keep_kernel
        in_specs.append(pl.BlockSpec((QUARTER, WIDE), lambda j, spot: (0, j)))
        operands.append(came)
        out_specs = [pl.BlockSpec((QUARTER // 2, WIDE), lambda j, spot: (0, at // WIDE + j))] * 2
        out_shape = [jax.ShapeDtypeStruct((QUARTER // 2, whole), BF)] * 2
        scratch = [pltpu.VMEM((QUARTER, WIDE), F32)]
        if into is not None:
            in_specs += [pl.BlockSpec(memory_space=pl.ANY)] * 2
            operands += into
            aliases = {6: 0, 7: 1}
    return pl.pallas_call(
        kernel,
        grid_spec=pltpu.PrefetchScalarGridSpec(
            num_scalar_prefetch=1, grid=(steps,), in_specs=in_specs, out_specs=out_specs, scratch_shapes=scratch
        ),
        out_shape=out_shape,
        input_output_aliases=aliases,
        cost_estimate=pl.CostEstimate(
            flops=4 * tokens * QUARTER * steps * WIDE, bytes_accessed=2 * tokens * (depth + 2 * width), transcendentals=0
        ),
    )(spot, *operands)


def sum_y_kernel(at_ref, held_ref, came_ref, *refs):
    outs, scr = refs[:-1], refs[-1]
    scr[...] = held_ref[...].astype(F32) + came_ref[...].astype(F32)
    tall = outs[0].shape[0]
    for n, out_ref in enumerate(outs):
        out_ref[...] = scr[pl.ds(pl.multiple_of(at_ref[n] * tall, tall), tall), :].astype(BF)


def sum_z_kernel(*refs):
    total = refs[0][...].astype(F32)
    for ref in refs[1:-1]:
        total += ref[...].astype(F32)
    refs[-1][...] = total.astype(BF)


def sum_y(held, came, order):
    tall, width = held.shape
    count = order.shape[0]
    wide = 2048
    spec = pl.BlockSpec((tall, wide), lambda j, at: (0, j))
    return pl.pallas_call(
        sum_y_kernel,
        grid_spec=pltpu.PrefetchScalarGridSpec(
            num_scalar_prefetch=1,
            grid=(width // wide,),
            in_specs=[spec, spec],
            out_specs=[pl.BlockSpec((tall // count, wide), lambda j, at: (0, j))] * count,
            scratch_shapes=[pltpu.VMEM((tall, wide), F32)],
        ),
        out_shape=[jax.ShapeDtypeStruct((tall // count, width), BF)] * count,
        cost_estimate=pl.CostEstimate(flops=tall * width, bytes_accessed=6 * tall * width, transcendentals=0),
    )(order, held, came)


def sum_z(parts):
    tall, width = parts[0].shape
    wide = 2048
    spec = pl.BlockSpec((tall, wide), lambda j: (0, j))
    return pl.pallas_call(
        sum_z_kernel,
        grid=(width // wide,),
        in_specs=[spec] * len(parts),
        out_specs=spec,
        out_shape=jax.ShapeDtypeStruct((tall, width), BF),
        cost_estimate=pl.CostEstimate(flops=4 * tall * width, bytes_accessed=10 * tall * width, transcendentals=0),
    )(*parts)


def place_kernel(spans, z_major, spot_ref, in_ref, *refs):
    outs = refs[-len(spans) :]
    count = in_ref.shape[0 if z_major else 1]
    share = in_ref.shape[2]
    for z in range(count):
        rows = pl.ds(pl.multiple_of(spot_ref[z] * share, share), share)
        for (at, subs, _, _), out_ref in zip(spans, outs, strict=True):
            wide = out_ref.shape[5]
            for k in range(subs):
                cols = slice(at + k * wide, at + (k + 1) * wide)
                piece = in_ref[z, 0, :, cols] if z_major else in_ref[0, z, :, cols]
                out_ref[0, 0, k, 0, rows, :] = piece.astype(F32)


def place_rows(gathered, z_major, spots, spans, layer, wholes):
    count, sides = gathered.shape[:2] if z_major else gathered.shape[1::-1]
    share, width = gathered.shape[2:]
    rows = count * share
    steps = width // WIDE if len(spans) == 1 and spans[0][3] is not None else 1
    part = width // steps
    block = (count, 1, share, part) if z_major else (1, count, share, part)
    shapes = [jax.ShapeDtypeStruct((LAYERS, 2, subs, 2, rows, wide), F32) for _, subs, wide, _ in spans]
    more = [] if wholes[0] is None else wholes

    def out_spec(span):
        _, subs, wide, first = span
        wide, at = (wide, 0) if first is None else (WIDE, first)
        return pl.BlockSpec(
            (1, 1, subs, 1, rows, wide), lambda b, j, spot: (layer, spot[count + b], 0, spot[count + sides + b], 0, at + j)
        )

    return pl.pallas_call(
        lambda *refs: place_kernel(spans, z_major, *refs),
        grid_spec=pltpu.PrefetchScalarGridSpec(
            num_scalar_prefetch=1,
            grid=(sides, steps),
            in_specs=[pl.BlockSpec(block, lambda b, j, spot: (0, b, 0, j) if z_major else (b, 0, 0, j))]
            + [pl.BlockSpec(memory_space=pl.ANY)] * len(more),
            out_specs=[out_spec(span) for span in spans],
        ),
        out_shape=shapes,
        input_output_aliases={n + 2: n for n in range(len(more))},
        cost_estimate=pl.CostEstimate(flops=0, bytes_accessed=6 * count * sides * share * width, transcendentals=0),
    )(spots, gathered, *more)


def build(sizes):
    group_axes = []
    reach = 1
    for name in reversed(ALL):
        if reach < GROUP:
            group_axes.insert(0, name)
            reach *= sizes[name]
    assert reach == GROUP
    group_axes = tuple(group_axes)
    total = sizes["z"] * sizes["y"] * sizes["c"] * sizes["x"]
    pairwise = sizes["x"] == 2 and sizes["z"] == 4

    def flip(value, axis, bit):
        return lax.ppermute(value, axis, [(i, i ^ bit) for i in range(sizes[axis])])

    def shift_groups(value, by):
        pairs = [(i, i + by * GROUP) for i in range(total) if 0 <= i + by * GROUP < total]
        return lax.ppermute(value, ALL, pairs)

    def all_weights(stacks, spot):
        if not pairwise:
            return [[lax.all_gather(w[layer], "x", axis=0, tiled=True) for w in stacks] for layer in range(LAYERS)]
        place = lax.axis_index(DP)
        result = []
        for layer in range(LAYERS):
            base = stacks[0].shape[1]

            def halved(w):
                tall = w.shape[1] // 2
                piece = lax.dynamic_slice(w, (layer, spot["c"] * tall, 0), (1, tall, w.shape[2]))[0]
                came = flip(piece, "x", 1)
                return came, flip(came, "c", 1)

            share = base // (total // 2)
            parts = [lax.dynamic_slice(w, (layer, place * share, 0), (1, share, w.shape[2]))[0] for w in stacks[1:3]]
            rest = jnp.concatenate(parts, axis=1)
            rest = flip(rest, "x", 1)
            rest = lax.all_gather(rest, DP, axis=0, tiled=True)
            result.append((halved(stacks[0]), rest, halved(stacks[3])))
        return result

    def swap_core(value):
        return flip(value, "c", 1)

    def rows_for_partner(rows, spot):
        quarter = rows.shape[1] // 4
        parts = [lax.dynamic_slice_in_dim(rows, (2 * n + 1 - spot["c"]) * quarter, quarter, 1) for n in range(2)]
        return jnp.concatenate(parts, axis=1)

    def grad_first(mine, theirs, cols, units, spot):
        cols2 = swap_core(cols)
        result = {}
        for unit in units:
            _, first, steps = UNITS[unit]
            away = block_grad(mine, theirs, cols, cols2, jnp.stack([1 - spot["x"], spot["c"]]), first, steps)
            came = flip(away, "x", 1)
            result[unit] = (mine, theirs, cols, cols2, came)
        return result

    def grad_group(firsts, group, layer, spot):
        units = GROUPS[group]
        whole = sum(firsts[unit][4].shape[1] for unit in units)
        here = jnp.stack([spot["x"], spot["c"], spot["y"]])
        pair = None
        at = 0
        for unit in units:
            _, first, steps = UNITS[unit]
            pair = block_grad(*firsts[unit][:4], here, first, steps, firsts[unit][4], pair, at, whole)
            at += firsts[unit][4].shape[1]
        held, away = pair
        came = flip(away, "y", 1)
        pieces = list(sum_y(held, came, jnp.stack([spot["z"] ^ n for n in range(4)])))
        for n in (1, 2, 3):
            pieces[n] = flip(pieces[n], "z", n)
        share = sum_z(pieces)
        if (group, layer) not in BY_HAND:
            gathered = lax.all_gather(share, DP, axis=0, tiled=False)
            spots = list(range(4)) + [b % 2 for b in range(4)] + [b // 2 for b in range(4)]
            return [(gathered.reshape((4, 4) + share.shape), True, jnp.array(spots, jnp.int32))]
        near = [share]
        for n in (1, 2, 3):
            near.append(flip(share, "z", n))
        near = jnp.stack(near)
        mine = jnp.stack([near, flip(near, "y", 1)])
        theirs = flip(mine, "c", 1)
        zs = [spot["z"] ^ n for n in range(4)]
        ys = [spot["y"], 1 - spot["y"]]
        return [(mine, False, jnp.stack(zs + [spot["c"]] * 2 + ys)), (theirs, False, jnp.stack(zs + [1 - spot["c"]] * 2 + ys))]

    def plain_grad(rows, cols, whole):
        part = lax.psum_scatter(tn(rows, cols).astype(BF), "x", scatter_dimension=0, tiled=True)
        part = lax.psum(part, DP).astype(F32)[None]
        return part if whole is None else jnp.concatenate([part, whole], axis=0)

    def total_vector(vector):
        if not pairwise:
            return lax.psum(vector, ALL)
        for axis, bit in (("c", 1), ("y", 1), ("x", 1), ("z", 1), ("z", 2)):
            came = flip(vector, axis, bit)
            vector = vector + came
        return vector

    def gather_group(value):
        for name in reversed(group_axes):
            step = 1
            while step < sizes[name]:
                came = flip(value, name, step)
                first = (lax.axis_index(name) // step) % 2 == 0
                value = jnp.concatenate([jnp.where(first, value, came), jnp.where(first, came, value)])
                step *= 2
        return value

    def swap_group(blocks):
        return lax.all_to_all(blocks, group_axes, split_axis=0, concat_axis=0, tiled=True)

    def to_heads(stacked):
        count, kinds, width = stacked.shape
        blocks = stacked.reshape(count, kinds, GROUP, width // GROUP).transpose(2, 0, 1, 3)
        return swap_group(blocks.reshape(GROUP * count, kinds * (width // GROUP)))

    def to_tokens(heads, kinds):
        swapped = lax.all_to_all(heads, group_axes, split_axis=0, concat_axis=0, tiled=True)
        count = heads.shape[0] // GROUP
        blocks = swapped.reshape(GROUP, count, kinds, heads.shape[1] // kinds)
        return blocks.transpose(1, 2, 0, 3).reshape(count, kinds * GROUP * (heads.shape[1] // kinds))

    def local(
        tokens,
        image_ids,
        pad_mask,
        cotangent,
        w_qkv,
        w_out,
        w_fc1,
        w_fc2,
        b_fc1,
        proj_bias,
        value_bias,
        ln_gain,
        ln_shift,
        layer_scale,
    ):
        count, width = tokens.shape
        halo = REACH * count
        spot = {name: lax.axis_index(name) for name in ALL}
        x = spot["x"]
        place = lax.axis_index(ALL)

        own_ids = jnp.where(
            pad_mask == 1, image_ids, (1 << 20) + place * count + jnp.arange(count, dtype=jnp.int32)
        )
        qid = gather_group(own_ids)
        group = place // GROUP
        before_ids = shift_groups(qid[-halo:], 1)
        after_ids = shift_groups(qid[:halo], -1)
        before_ids = jnp.where(group == 0, -1, before_ids)
        after_ids = jnp.where(group == total // GROUP - 1, -1, after_ids)
        kid = jnp.concatenate([before_ids, qid, after_ids])
        span = kid.shape[0]
        qblk = qid.reshape(GROUP, count)
        where = jnp.arange(span, dtype=jnp.int32)[None]
        first = jnp.min(jnp.where(kid[None] == qblk[:, :1], where, span), axis=1)
        last = jnp.max(jnp.where(kid[None] == qblk[:, -1:], where, 0), axis=1)
        lo = first // LANES
        hi = last // LANES + 1
        qid_col = qid[:, None]
        qid_row = jnp.concatenate([qblk, qblk], axis=1)[:, None, :]
        kid_col = kid[:, None]
        kid_row = kid.reshape(span // LANES, 1, LANES)

        vectors = (b_fc1, proj_bias, value_bias, ln_gain, ln_shift, layer_scale)
        packed = jnp.concatenate([v.reshape(-1) for v in vectors])
        if pairwise:
            came = flip(packed, "x", 1)
            packed = jnp.stack([jnp.where(x == 0, packed, came), jnp.where(x == 0, came, packed)])
        else:
            packed = lax.all_gather(packed, "x", axis=0, tiled=False)
        shards = packed.shape[0]
        full = []
        at = 0
        for v in vectors:
            part = packed[:, at : at + v.size].reshape((shards,) + v.shape)
            at += v.size
            part = jnp.moveaxis(part, 0, -2)
            full.append(part.reshape(v.shape[:-1] + (shards * v.shape[-1],)).astype(F32))
        fc1_bias, bias, value_shift, gain, shift, scale = full

        weights = all_weights((w_qkv, w_out, w_fc1, w_fc2), spot)
        hidden_size = fc1_bias.shape[1]
        mat_at = (0, 0, width)
        whole_row = lambda size: pl.BlockSpec((count, size), lambda j, x: (0, 0))
        col_block = lambda size: pl.BlockSpec((count, size), lambda j, x: (0, j))
        kind = jax.ShapeDtypeStruct
        half = width // 2
        near, far = x * half, (1 - x) * half
        two_starts = jnp.stack([near, far])
        qkv_starts = jnp.stack([near] + [far + n * (half // 2) for n in (spot["c"], 1 - spot["c"])])
        fc2_subs = hidden_size // width
        fc2_starts = fc2_subs * qkv_starts

        residual = tokens.astype(F32)
        kept = []
        for layer in range(LAYERS):
            normed_in = layer_norm(residual, gain[layer, 0], shift[layer, 0]).astype(BF)
            added = jnp.concatenate([bias[layer, 0], jnp.zeros_like(bias[layer, 0]), value_shift[layer]])
            if pairwise:
                first_w, rest_w, last_w = weights[layer]
                heads = product(
                    qkv_kernel, normed_in, w_qkv, layer, [(w, half // 2, 0) for w in first_w], qkv_starts, width, added,
                    pl.BlockSpec((GROUP, count, 2 * HD), lambda j, x: (0, 0, j)), kind((GROUP, count, 6 * HD), BF),
                )
                heads = swap_group(heads.reshape(GROUP * count, 6 * HD))
            else:
                projected = nn(normed_in, weights[layer][0])
                heads = to_heads((projected + added).astype(BF).reshape(count, 3, width))
            kv_own = heads[:, 2 * HD :]
            before = shift_groups(kv_own[-halo:], 1)
            after = shift_groups(kv_own[:halo], -1)
            kv_win = jnp.concatenate([before, kv_own, after], axis=0)
            mixed_heads, mixed_f, lse = attn_fwd(heads, kv_win, qid_col, kid_row, lo, hi)
            mixed = to_tokens(mixed_heads, 1)
            if pairwise:
                branch_attn = product(
                    plain_kernel, mixed, w_out, layer, [(rest_w, half, mat_at[1])], two_starts, width // 2, bias[layer, 1],
                    col_block(width // 2), kind((count, width), F32),
                )
            else:
                branch_attn = nn(mixed, weights[layer][1]) + bias[layer, 1]
            middle = residual + scale[layer, 0] * branch_attn
            normed_mid = layer_norm(middle, gain[layer, 1], shift[layer, 1]).astype(BF)
            if pairwise:
                active, slope = product(
                    fc1_kernel, normed_mid, w_fc1, layer, [(rest_w, half, mat_at[2])], two_starts, width // 2, fc1_bias[layer],
                    [col_block(width // 2)] * 2, [kind((count, hidden_size), BF)] * 2,
                )
                branch_mlp = product(
                    plain_kernel, active, w_fc2, layer, [(w, hidden_size // 4, 0) for w in last_w],
                    fc2_starts, width // 2, bias[layer, 2], col_block(width // 2), kind((count, width), F32),
                )
            else:
                active, slope = gelu_parts(nn(normed_mid, weights[layer][2]) + fc1_bias[layer])
                active, slope = active.astype(BF), slope.astype(BF)
                branch_mlp = nn(active, weights[layer][3]) + bias[layer, 2]
            partner = (None,) * 4
            if pairwise:
                partner = tuple(
                    swap_core(rows_for_partner(t, spot)) for t in (normed_in, mixed, normed_mid, active)
                )
            kept.append(
                (residual, normed_in, heads, kv_win, mixed_f, lse, mixed, branch_attn, middle, normed_mid, slope, active, branch_mlp, partner)
            )
            residual = middle + scale[layer, 1] * branch_mlp
        output = residual.astype(BF)

        grad_res = cotangent.astype(F32)
        big = [None] * 4
        small = [None] * LAYERS
        for layer in reversed(range(LAYERS)):
            (
                residual, normed_in, heads, kv_win, mixed_f, lse, mixed, branch_attn, middle, normed_mid, slope, active, branch_mlp, partner
            ) = kept[layer]
            g_scale_mlp = jnp.sum(grad_res * branch_mlp, axis=0)
            g_mlp = (scale[layer, 1] * grad_res).astype(BF)
            g_bias_mlp = jnp.sum(g_mlp.astype(F32), axis=0)
            if pairwise:
                first_w, rest_w, last_w = weights[layer]
                sub = hidden_size // 2 // (hidden_size // width)
                g_hidden, g_fc1_bias = pl.pallas_call(
                    gact_kernel,
                    grid_spec=pltpu.PrefetchScalarGridSpec(
                        num_scalar_prefetch=1,
                        grid=(hidden_size // width,),
                        in_specs=[
                            whole_row(width),
                            pl.BlockSpec((1, sub, width), lambda k, x: (layer, k, 0)),
                            *[pl.BlockSpec((sub // 2, width), lambda k, x: (k, 0))] * 2,
                            whole_row(hidden_size),
                        ],
                        out_specs=[whole_row(hidden_size), pl.BlockSpec((1, hidden_size), lambda k, x: (0, 0))],
                    ),
                    out_shape=[kind((count, hidden_size), BF), kind((1, hidden_size), F32)],
                    cost_estimate=pl.CostEstimate(
                        flops=2 * count * width * hidden_size, bytes_accessed=2 * width * hidden_size, transcendentals=0
                    ),
                )(fc2_starts, g_mlp, w_fc2, *last_w, slope)
                g_fc1_bias = g_fc1_bias[0]
                firsts = grad_first(active, partner[FC2], g_mlp, (FC2A, FC2B), spot)
                g_normed_mid = product_back(
                    dx_plain_kernel, g_hidden, col_block(width), w_fc1, layer, [(rest_w, half, mat_at[2])], two_starts, width,
                    whole_row(width), kind((count, width), F32),
                )
                firsts |= grad_first(normed_mid, partner[FC1], g_hidden, (FC1A, FC1B), spot)
            else:
                g_hidden = (nt(g_mlp, weights[layer][3]) * slope.astype(F32)).astype(BF)
                g_fc1_bias = jnp.sum(g_hidden.astype(F32), axis=0)
                g_normed_mid = nt(g_hidden, weights[layer][2])
                big[3] = plain_grad(active, g_mlp, big[3])
                big[2] = plain_grad(normed_mid, g_hidden, big[2])
            _, norm_pull = jax.vjp(layer_norm, middle, gain[layer, 1], shift[layer, 1])
            g_middle, g_gain_mid, g_shift_mid = norm_pull(g_normed_mid)
            g_middle = grad_res + g_middle
            g_scale_attn = jnp.sum(g_middle * branch_attn, axis=0)
            g_attn = (scale[layer, 0] * g_middle).astype(BF)
            g_bias_attn = jnp.sum(g_attn.astype(F32), axis=0)
            if pairwise:
                g_mixed = product_back(
                    dx_out_kernel, g_attn, col_block(width // 2), w_out, layer, [(rest_w, half, mat_at[1])], two_starts, width // 2,
                    pl.BlockSpec((GROUP, count, 2 * HD), lambda j, x: (0, 0, 0)), kind((GROUP, count, 2 * HD), BF),
                    [pltpu.VMEM((count, width), F32)],
                )
                g_heads = swap_group(g_mixed.reshape(GROUP * count, 2 * HD))
                firsts |= grad_first(mixed, partner[OUT], g_attn, (NOUT,), spot)
            else:
                g_heads = to_heads(nt(g_attn, weights[layer][1]).astype(BF)[:, None, :])
                big[1] = plain_grad(mixed, g_attn, big[1])
            g_q, g_kv, g_before, g_after = attn_bwd(heads, kv_win, g_heads, qid_row, kid_col, lse, mixed_f, lo, hi)
            from_after = shift_groups(g_before, -1).astype(F32)
            from_before = shift_groups(g_after, 1).astype(F32)
            rest = GROUP * count - halo
            g_kv = g_kv + jnp.pad(from_after, ((rest, 0), (0, 0))) + jnp.pad(from_before, ((0, rest), (0, 0)))
            g_qkv_heads = jnp.concatenate([g_q, g_kv.astype(BF)], axis=1)
            if pairwise:
                g_swapped = swap_group(g_qkv_heads).reshape(GROUP, count, 6 * HD)
                g_normed_in, g_proj = product_back(
                    dx_qkv_kernel, g_swapped, pl.BlockSpec((GROUP, count, 2 * HD), lambda j, x: (0, 0, j)),
                    w_qkv, layer, [(w, half // 2, 0) for w in first_w], qkv_starts, width,
                    [whole_row(width), col_block(width)], [kind((count, width), F32), kind((count, 3 * width), BF)],
                )
                firsts |= grad_first(normed_in, partner[QKV], g_proj, (NQKV,) if GQ in USED[layer] else (NQ, NKV), spot)
                out_span, qkv_wide = (0, 1, width, None), 3 * width
                spans = {
                    G2: ((FC2, (0, fc2_subs, width, None)),),
                    G1: ((FC1, (0, 1, hidden_size, None)),),
                    GQ: ((OUT, out_span), (QKV, (width, 1, qkv_wide, None))),
                    GA: ((OUT, out_span), (QKV, (width, 1, qkv_wide, 0))),
                    GB: ((QKV, (0, 1, qkv_wide, 1)),),
                }
                for group in USED[layer]:
                    mats, cut = zip(*spans[group], strict=True)
                    for gathered, z_major, spots in grad_group(firsts, group, layer, spot):
                        placed = place_rows(gathered, z_major, spots, cut, layer, [big[m] for m in mats])
                        for m, value in zip(mats, placed, strict=True):
                            big[m] = value
            else:
                g_proj = to_tokens(g_qkv_heads, 3)
                g_normed_in = nt(g_proj, weights[layer][0])
                big[0] = plain_grad(normed_in, g_proj, big[0])
            g_bias_query = jnp.sum(g_proj[:, :width].astype(F32), axis=0)
            g_value = jnp.sum(g_proj[:, 2 * width :].astype(F32), axis=0)
            _, first_pull = jax.vjp(layer_norm, residual, gain[layer, 0], shift[layer, 0])
            g_input, g_gain_in, g_shift_in = first_pull(g_normed_in)
            grad_res = g_middle + g_input
            small[layer] = (
                jnp.concatenate(
                    [
                        g_fc1_bias,
                        g_bias_query,
                        g_bias_attn,
                        g_bias_mlp,
                        g_value,
                        g_gain_in,
                        g_gain_mid,
                        g_shift_in,
                        g_shift_mid,
                        g_scale_attn,
                        g_scale_mlp,
                    ]
                )
            )

        stacked = [b.reshape(w.shape) for b, w in zip(big, (w_qkv, w_out, w_fc1, w_fc2), strict=True)]
        sums = total_vector(jnp.stack(small))
        at = 0
        for v in vectors:
            lead = v.shape[1:-1]
            wide = shards * v.shape[-1]
            size = wide
            for n in lead:
                size *= n
            part = sums[:, at : at + size].reshape((LAYERS,) + lead + (wide,))
            at += size
            stacked.append(lax.dynamic_slice_in_dim(part, x * v.shape[-1], v.shape[-1], part.ndim - 1))
        return (output, grad_res.astype(BF), *stacked)

    return local


def solution(mesh):
    dp, fsdp = mesh.shape["dp"], mesh.shape["fsdp"]
    sizes = {"z": dp // 4, "y": 2, "c": 2, "x": fsdp}
    fine = Mesh(mesh.devices.reshape(tuple(sizes.values())), ALL)
    token = P(ALL)
    rows = P(ALL, None)
    vec2, vec3, mat = P(None, "x"), P(None, None, "x"), P(None, "x", None)
    in_specs = (rows, token, token, rows, mat, mat, mat, mat, vec2, vec3, vec2, vec3, vec3, vec3)
    out_specs = (rows, rows, mat, mat, mat, mat, vec2, vec3, vec2, vec3, vec3, vec3)
    return jax.shard_map(build(sizes), mesh=fine, in_specs=in_specs, out_specs=out_specs, check_vma=False)
```

time: 2970 us -> 1280 us (0.43)
  waiting for transfers between devices: 1550 us -> 527 us
  matrix products: 488 us -> 0 us
  Pallas kernels: 0 us -> 408 us
  blocking collectives: 216 us -> 23.9 us
  other arithmetic: 222 us -> 66.7 us
  local copies, waits for them, and re-layouts: 180 us -> 49 us
  starting transfers between devices: 283 us -> 170 us
    reduce_scatter x8 -> x0, waiting for transfers between devices: 493 us -> none  [the longest x2 204 us: local(): lax.psum_scatter(grad_fc1.astype(jnp.bfloat16), 'fsdp', scatter_dimension...]
    dot_general x80 -> x0, matrix products: 488 us -> none  [the longest x16 132 us: group_step(): jnp.einsum('qhd,khd->hqk', query_grp, key_grp, preferred_element_type=jnp...]
    pallas_call x0 -> x70, Pallas kernels: none -> 408 us  [the longest x26 103 us: block_grad(): pl.pallas_call(kernel, grid_spec=pltpu.PrefetchScalarGridSpec(num_scalar_...]
    psum x1 -> x0, waiting for transfers between devices: 375 us -> none  [local(): lax.psum(shard_sums[0].astype(jnp.bfloat16), 'dp').astype(jnp.float32)]
    all_gather x12 -> x0, blocking collectives: 144 us -> none  [the longest x2 97.8 us: gather_forward(): lax.all_gather(b_fc1[layer_idx], 'fsdp', axis=0, tiled=True)]
    ppermute x60 -> x101, starting transfers between devices: 281 us -> 141 us  [the longest x91 109 us: flip(): return lax.ppermute(value, axis, [(i, i ^ bit) for i in range(sizes[axis])])]
    unnamed x33 -> x6, waiting for transfers between devices: 95.5 us -> 0.1 us
    slice x27 -> x14, local copies, waits for them, and re-layouts: 92.2 us -> 1.25 us  [the longest x1 0.84 us: local(): bias[layer, 2]]
  transfers between devices with their start and end apart: 85 -> 114, of which waited for: 40 -> 48; matrix products, arithmetic and copies ran while one was open for 22% -> 7% of each run, Pallas kernels for 0% -> 31%
where the time goes in v1:
time: 1280 us; the launch traced here: 1260 us
  waiting for transfers between devices  527 us (41%)
  Pallas kernels  408 us (32%)
  starting transfers between devices  170 us (13%)
  other arithmetic  66.7 us (5%)
  local copies, waits for them, and re-layouts  49 us (4%)
  blocking collectives  23.9 us (2%)
  between operations  16 us (1%)
    ppermute x91, waiting for transfers between devices, flip(): return lax.ppermute(value, axis, [(i, i ^ bit) for i in range(sizes[axis])])  407 us
    ppermute x91, starting transfers between devices, flip(): return lax.ppermute(value, axis, [(i, i ^ bit) for i in range(sizes[axis])])  109 us
    pallas_call x26, Pallas kernels, block_grad(): pl.pallas_call(kernel, grid_spec=pltpu.PrefetchScalarGridSpec(num_scalar_...  103 us
    ppermute x10, waiting for transfers between devices, shift_groups(): return lax.ppermute(value, ALL, pairs)  70.9 us
    pallas_call x2, Pallas kernels, attn_bwd(): pl.pallas_call(attn_bwd_kernel, grid_spec=pltpu.PrefetchScalarGridSpec(nu...  65.5 us
    pallas_call x8, Pallas kernels, product(): pl.pallas_call(kernel, grid_spec=pltpu.PrefetchScalarGridSpec(num_scalar_...  57.5 us
    pallas_call x10, Pallas kernels, place_rows(): pl.pallas_call(lambda *refs: place_kernel(spans, z_major, *refs), grid_sp...  49.4 us
    pallas_call x6, Pallas kernels, product_back(): pl.pallas_call(kernel, grid_spec=pltpu.PrefetchScalarGridSpec(num_scalar_...  42.8 us
  transfers between devices with their start and end apart: 114, of which 48 were waited for; matrix products, arithmetic and copies ran while one was open for 7% of the time, Pallas kernels for 31%

profile of v1, /device:TPU:0, one launch (start us, length us, event | category | flops | bytes accessed | tf_op | source)
XLA Modules:
  0.0 1259.8 jit_solution(3946598963078965967)
XLA Ops:
  39.9 61.6 %collective-permute-done.6.refs_0_ = bf16[256,3072]{1,0:T(8,128)(2,1)S(1)} collective-permute-done((bf16[256,3072]{1,0:T(8,128)(2,1)}, bf16[256,3072]{1,0:T(8,128)(2,1)S(1)}, u32[]{:S(2)}, u32[]{:S(2)}) %collective-permute-start.6) | collective-permute-done | bytes 1572896 | tf_op jit(solution)/shard_map/ppermute | solution.py:559
  127.3 32.9 %all-to-all-done = bf16[8,256,384]{2,1,0:T(8,128)(2,1)S(1)} async-done(((bf16[8,256,384]{2,1,0:T(8,128)(2,1)}), bf16[8,256,384]{2,1,0:T(8,128)(2,1)S(1)}, u32[]{:S(2)}, u32[]{:S(2)}) %all-to-all-start) | async-done | bytes 1572896 | tf_op jit(solution)/shard_map/all_to_all | solution.py:659
  166.3 27.6 %collective-permute-done.8 = bf16[1536,256]{1,0:T(8,128)(2,1)S(1)} collective-permute-done((bf16[1536,256]{1,0:T(8,128)(2,1)S(1)}, bf16[1536,256]{1,0:T(8,128)(2,1)S(1)}, u32[]{:S(2)}, u32[]{:S(2)}) %collective-permute-start.8) | collective-permute-done | bytes 786464 | tf_op jit(solution)/shard_map/ppermute | solution.py:563
  198.3 18.4 %attn_fwd.2 = (bf16[2048,128]{1,0:T(8,128)(2,1)}, f32[2048,128]{1,0:T(8,128)}, f32[8,1,512]{2,1,0:T(1,128)}) custom-call(s32[8]{0:T(128)} %get-tuple-element.358.lo_ref, s32[8]{0:T(128)} %get-tuple-element.359.hi_ref, bf16[2048,384]{1,0:T(8,128)(2,1)} %bitcast.152, bf16[5120,256]{1,0:T(8,128)(2,1)} %pad_maximum_fusion.k_ref.v_ref, ...), custom_call_target="tpu_custom_call" | custom-call | flops 3758096384 | bytes 4718592 | tf_op jit(solution)/shard_map/attn_fwd/pallas_call | solution.py:119
  264.8 23.9 %all_to_all.68 = bf16[8,256,384]{2,1,0:T(8,128)(2,1)S(1)} all-to-all(bf16[8,256,384]{2,1,0:T(8,128)(2,1)} %shard_map.269), channel_id=1, replica_groups=mesh['z'=4,'y'=2,'c'=2,'x'=2] {'y','c','x'}, dimensions={0} | all-to-all | bytes 3145728 | tf_op jit(solution)/shard_map/all_to_all | solution.py:659
  294.1 15.2 %collective-permute-done.15 = bf16[1536,256]{1,0:T(8,128)(2,1)S(1)} collective-permute-done((bf16[1536,256]{1,0:T(8,128)(2,1)S(1)}, bf16[1536,256]{1,0:T(8,128)(2,1)S(1)}, u32[]{:S(2)}, u32[]{:S(2)}) %collective-permute-start.15) | collective-permute-done | bytes 786464 | tf_op jit(solution)/shard_map/ppermute | solution.py:563
  316.1 18.4 %attn_fwd.3 = (bf16[2048,128]{1,0:T(8,128)(2,1)}, f32[2048,128]{1,0:T(8,128)}, f32[8,1,512]{2,1,0:T(1,128)}) custom-call(s32[8]{0:T(128)} %get-tuple-element.358.lo_ref, s32[8]{0:T(128)} %get-tuple-element.359.hi_ref, bf16[2048,384]{1,0:T(8,128)(2,1)} %bitcast.156, bf16[5120,256]{1,0:T(8,128)(2,1)} %pad_maximum_fusion.1.k_ref.v_ref, ...), custom_call_target="tpu_custom_call" | custom-call | flops 3758096384 | bytes 4718592 | tf_op jit(solution)/shard_map/attn_fwd/pallas_call | solution.py:119
  382.7 18.8 %collective-permute-done.91.came_ref = bf16[256,2048]{1,0:T(8,128)(2,1)} collective-permute-done((bf16[256,2048]{1,0:T(8,128)(2,1)}, bf16[256,2048]{1,0:T(8,128)(2,1)}, u32[]{:S(2)}, u32[]{:S(2)}) %collective-permute-start.91) | collective-permute-done | bytes 1048608 | tf_op jit(solution)/shard_map/ppermute | solution.py:559
  405.6 18.4 %collective-permute-done.90.came_ref = bf16[256,2048]{1,0:T(8,128)(2,1)} collective-permute-done((bf16[256,2048]{1,0:T(8,128)(2,1)}, bf16[256,2048]{1,0:T(8,128)(2,1)}, u32[]{:S(2)}, u32[]{:S(2)}) %collective-permute-start.90) | collective-permute-done | bytes 1048608 | tf_op jit(solution)/shard_map/ppermute | solution.py:559
  429.3 22.6 %collective-permute-done.92.came_ref = bf16[128,4096]{1,0:T(8,128)(2,1)} collective-permute-done((bf16[128,4096]{1,0:T(8,128)(2,1)}, bf16[128,4096]{1,0:T(8,128)(2,1)}, u32[]{:S(2)}, u32[]{:S(2)}) %collective-permute-start.92) | collective-permute-done | bytes 1048608 | tf_op jit(solution)/shard_map/ppermute | solution.py:559
  464.8 12.9 %collective-permute-done.94.refs_2_ = bf16[32,4096]{1,0:T(8,128)(2,1)} collective-permute-done((bf16[32,4096]{1,0:T(8,128)(2,1)}, bf16[32,4096]{1,0:T(8,128)(2,1)}, u32[]{:S(2)}, u32[]{:S(2)}) %collective-permute-start.94) | collective-permute-done | bytes 262176 | tf_op jit(solution)/shard_map/ppermute | solution.py:559
  530.1 32.8 %attn_bwd.2 = (bf16[2048,128]{1,0:T(8,128)(2,1)}, f32[2048,256]{1,0:T(8,128)}, bf16[1536,256]{1,0:T(8,128)(2,1)}, bf16[1536,256]{1,0:T(8,128)(2,1)}) custom-call(s32[8]{0:T(128)} %get-tuple-element.358.lo_ref, s32[8]{0:T(128)} %get-tuple-element.359.hi_ref, bf16[2048,384]{1,0:T(8,128)(2,1)} %bitcast.157, bf16[5120,256]{1,0:T(8,128)(2,1)} %pad_maximum_fusion.1.k_ref.v_ref, ...), custom_call_target="tpu_custom_call" | custom-call | flops 9395240960 | bytes 11010048 | tf_op jit(solution)/shard_map/attn_bwd/pallas_call | solution.py:216
  595.2 20.4 %collective-permute-done.71.came_ref = bf16[128,4096]{1,0:T(8,128)(2,1)} collective-permute-done((bf16[128,4096]{1,0:T(8,128)(2,1)}, bf16[128,4096]{1,0:T(8,128)(2,1)}, u32[]{:S(2)}, u32[]{:S(2)}) %collective-permute-start.71) | collective-permute-done | bytes 1048608 | tf_op jit(solution)/shard_map/ppermute | solution.py:559
  718.3 16.9 %collective-permute-done.61.came_ref = bf16[256,2048]{1,0:T(8,128)(2,1)} collective-permute-done((bf16[256,2048]{1,0:T(8,128)(2,1)}, bf16[256,2048]{1,0:T(8,128)(2,1)}, u32[]{:S(2)}, u32[]{:S(2)}) %collective-permute-start.61) | collective-permute-done | bytes 1048608 | tf_op jit(solution)/shard_map/ppermute | solution.py:559
  754.2 14.6 %collective-permute-done.63.came_ref = bf16[128,4096]{1,0:T(8,128)(2,1)} collective-permute-done((bf16[128,4096]{1,0:T(8,128)(2,1)}, bf16[128,4096]{1,0:T(8,128)(2,1)}, u32[]{:S(2)}, u32[]{:S(2)}) %collective-permute-start.63) | collective-permute-done | bytes 1048608 | tf_op jit(solution)/shard_map/ppermute | solution.py:559
  803.4 32.7 %attn_bwd.3 = (bf16[2048,128]{1,0:T(8,128)(2,1)}, f32[2048,256]{1,0:T(8,128)}, bf16[1536,256]{1,0:T(8,128)(2,1)}, bf16[1536,256]{1,0:T(8,128)(2,1)}) custom-call(s32[8]{0:T(128)} %get-tuple-element.358.lo_ref, s32[8]{0:T(128)} %get-tuple-element.359.hi_ref, bf16[2048,384]{1,0:T(8,128)(2,1)} %bitcast.153, bf16[5120,256]{1,0:T(8,128)(2,1)} %pad_maximum_fusion.k_ref.v_ref, ...), custom_call_target="tpu_custom_call" | custom-call | flops 9395240960 | bytes 11010048 | tf_op jit(solution)/shard_map/attn_bwd/pallas_call | solution.py:216
  850.8 13.1 %collective-permute-done.22 = bf16[1536,256]{1,0:T(8,128)(2,1)} collective-permute-done((bf16[1536,256]{1,0:T(8,128)(2,1)}, bf16[1536,256]{1,0:T(8,128)(2,1)}, u32[]{:S(2)}, u32[]{:S(2)}) %collective-permute-start.22) | collective-permute-done | bytes 786464 | tf_op jit(solution)/shard_map/ppermute | solution.py:563
  896.2 19.3 %collective-permute-done.78.came_ref = bf16[256,2048]{1,0:T(8,128)(2,1)} collective-permute-done((bf16[256,2048]{1,0:T(8,128)(2,1)}, bf16[256,2048]{1,0:T(8,128)(2,1)}, u32[]{:S(2)}, u32[]{:S(2)}) %collective-permute-start.78) | collective-permute-done | bytes 1048608 | tf_op jit(solution)/shard_map/ppermute | solution.py:559
  919.6 18.4 %collective-permute-done.77.came_ref = bf16[256,2048]{1,0:T(8,128)(2,1)} collective-permute-done((bf16[256,2048]{1,0:T(8,128)(2,1)}, bf16[256,2048]{1,0:T(8,128)(2,1)}, u32[]{:S(2)}, u32[]{:S(2)}) %collective-permute-start.77) | collective-permute-done | bytes 1048608 | tf_op jit(solution)/shard_map/ppermute | solution.py:559
  955.7 15.9 %collective-permute-done.51.came_ref = bf16[256,3072]{1,0:T(8,128)(2,1)S(1)} collective-permute-done((bf16[256,3072]{1,0:T(8,128)(2,1)}, bf16[256,3072]{1,0:T(8,128)(2,1)S(1)}, u32[]{:S(2)}, u32[]{:S(2)}) %collective-permute-start.51) | collective-permute-done | bytes 1572896 | tf_op jit(solution)/shard_map/ppermute | solution.py:559
  989.2 13.9 %collective-permute-done.55.came_ref = bf16[128,4096]{1,0:T(8,128)(2,1)} collective-permute-done((bf16[128,4096]{1,0:T(8,128)(2,1)}, bf16[128,4096]{1,0:T(8,128)(2,1)}, u32[]{:S(2)}, u32[]{:S(2)}) %collective-permute-start.55) | collective-permute-done | bytes 1048608 | tf_op jit(solution)/shard_map/ppermute | solution.py:559
  1037.2 13.4 %collective-permute-done.57.refs_2_ = bf16[32,4096]{1,0:T(8,128)(2,1)} collective-permute-done((bf16[32,4096]{1,0:T(8,128)(2,1)}, bf16[32,4096]{1,0:T(8,128)(2,1)}, u32[]{:S(2)}, u32[]{:S(2)}) %collective-permute-start.57) | collective-permute-done | bytes 262176 | tf_op jit(solution)/shard_map/ppermute | solution.py:559
  1105.7 12.7 %collective-permute-done.40.came_ref = bf16[128,2048]{1,0:T(8,128)(2,1)} collective-permute-done((bf16[128,2048]{1,0:T(8,128)(2,1)}, bf16[128,2048]{1,0:T(8,128)(2,1)}, u32[]{:S(2)}, u32[]{:S(2)}) %collective-permute-start.40) | collective-permute-done | bytes 524320 | tf_op jit(solution)/shard_map/ppermute | solution.py:559
  1147.9 13.2 %collective-permute-done.29.refs_2_ = bf16[32,2048]{1,0:T(8,128)(2,1)S(1)} collective-permute-done((bf16[32,2048]{1,0:T(8,128)(2,1)}, bf16[32,2048]{1,0:T(8,128)(2,1)S(1)}, u32[]{:S(2)}, u32[]{:S(2)}) %collective-permute-start.29) | collective-permute-done | bytes 131104 | tf_op jit(solution)/shard_map/ppermute | solution.py:559
  (649 shorter events, 736.0 us)
Async XLA Ops:
  7.3 223.3 %all-gather.11.cloned.1.call-start = ((), (), s32[]{:S(2)}) async-start(), calls=%async_computation.8 | async-start | bytes 5570560 | tf_op jit(solution)/shard_map/all_gather | solution.py:583
  23.2 103.3 %collective-permute-start.17 = (bf16[32,5120]{1,0:T(8,128)(2,1)S(1)}, bf16[32,5120]{1,0:T(8,128)(2,1)S(1)}, u32[]{:S(2)}, u32[]{:S(2)}) collective-permute-start(bf16[32,5120]{1,0:T(8,128)(2,1)S(1)} %pad_maximum_fusion.13), channel_id=1, source_target_pairs={{0,1},{1,0},{2,3},{3,2},{4,5},{5,4},{6,7},{7,6},{8,9},{9,8},{10,11... | collective-permute-start | bytes 983048 | tf_op jit(solution)/shard_map/ppermute | solution.py:559
  28.9 192.1 %collective-permute-start.13 = (bf16[256,3072]{1,0:T(8,128)(2,1)}, bf16[256,3072]{1,0:T(8,128)(2,1)}, u32[]{:S(2)}, u32[]{:S(2)}) collective-permute-start(bf16[256,3072]{1,0:T(8,128)(2,1)} %get-tuple-element.285), channel_id=1, source_target_pairs={{0,1},{1,0},{2,3},{3,2},{4,5},{5,4},{6,7},{7,6},{8,9},{9,8},{10,11... | collective-permute-start | bytes 4718600 | tf_op jit(solution)/shard_map/ppermute | solution.py:559
  29.1 72.3 %collective-permute-start.6 = (bf16[256,3072]{1,0:T(8,128)(2,1)}, bf16[256,3072]{1,0:T(8,128)(2,1)S(1)}, u32[]{:S(2)}, u32[]{:S(2)}) collective-permute-start(bf16[256,3072]{1,0:T(8,128)(2,1)} %get-tuple-element.286), channel_id=1, source_target_pairs={{0,1},{1,0},{2,3},{3,2},{4,5},{5,4},{6,7},{7,6},{8,9},{9,8},{10,11... | collective-permute-start | bytes 4718600 | tf_op jit(solution)/shard_map/ppermute | solution.py:559
  37.3 127.9 %collective-permute-start.11 = (bf16[1024,1024]{1,0:T(8,128)(2,1)}, bf16[1024,1024]{1,0:T(8,128)(2,1)}, u32[]{:S(2)}, u32[]{:S(2)}) collective-permute-start(bf16[1024,1024]{1,0:T(8,128)(2,1)} %get-tuple-element.282), channel_id=1, source_target_pairs={{0,1},{1,0},{2,3},{3,2},{4,5},{5,4},{6,7},{7,6},{8,9},{9,8},{10,11... | collective-permute-start | bytes 6291464 | tf_op jit(solution)/shard_map/ppermute | solution.py:559
  37.8 78.8 %collective-permute-start.3 = (s32[1024]{0:T(1024)S(1)}, s32[1024]{0:T(1024)S(1)}, u32[]{:S(2)}, u32[]{:S(2)}) collective-permute-start(s32[1024]{0:T(1024)S(1)} %pad_add_fusion.3), channel_id=1, source_target_pairs={{0,4},{4,0},{1,5},{5,1},{2,6},{6,2},{3,7},{7,3},{8,12},{12,8},{9,1... | collective-permute-start | bytes 12296 | tf_op jit(solution)/shard_map/ppermute | solution.py:559
  115.8 232.5 %all-gather.13.cloned.1.call-start = ((), (), s32[]{:S(2)}) async-start(), calls=%async_computation.9 | async-start | bytes 5570560 | tf_op jit(solution)/shard_map/all_gather | solution.py:583
  165.3 82.8 %collective-permute-start.12 = (bf16[1024,1024]{1,0:T(8,128)(2,1)}, bf16[1024,1024]{1,0:T(8,128)(2,1)}, u32[]{:S(2)}, u32[]{:S(2)}) collective-permute-start(bf16[1024,1024]{1,0:T(8,128)(2,1)} %collective-permute-done.11.refs_0_), channel_id=1, source_target_pairs={{0,2},{2,0},{1,3},{3,1},{4,6},{6,4},{5,7},{7,5},{8,10},{10,8},{9,1... | collective-permute-start | bytes 6291464 | tf_op jit(solution)/shard_map/ppermute | solution.py:559
  338.0 864.4 %all-gather.21.cloned.1.call-start = ((), (), s32[]{:S(2)}) async-start(), calls=%async_computation.13 | async-start | bytes 4456448 | tf_op jit(solution)/shard_map/all_gather | solution.py:622
  381.0 98.7 %collective-permute-start.18 = (bf16[1024,1024]{1,0:T(8,128)(2,1)}, bf16[1024,1024]{1,0:T(8,128)(2,1)}, u32[]{:S(2)}, u32[]{:S(2)}) collective-permute-start(bf16[1024,1024]{1,0:T(8,128)(2,1)} %get-tuple-element.281), channel_id=1, source_target_pairs={{0,1},{1,0},{2,3},{3,2},{4,5},{5,4},{6,7},{7,6},{8,9},{9,8},{10,11... | collective-permute-start | bytes 6291464 | tf_op jit(solution)/shard_map/ppermute | solution.py:559
  524.4 52.3 %collective-permute-start.69 = (bf16[256,2048]{1,0:T(8,128)(2,1)}, bf16[256,2048]{1,0:T(8,128)(2,1)}, u32[]{:S(2)}, u32[]{:S(2)}) collective-permute-start(bf16[256,2048]{1,0:T(8,128)(2,1)} %shard_map.308), channel_id=1, source_target_pairs={{0,1},{1,0},{2,3},{3,2},{4,5},{5,4},{6,7},{7,6},{8,9},{9,8},{10,11... | collective-permute-start | bytes 3145736 | tf_op jit(solution)/shard_map/ppermute | solution.py:559
  590.8 57.2 %all-to-all-start.5 = ((bf16[8,256,384]{2,1,0:T(8,128)(2,1)}), bf16[8,256,384]{2,1,0:T(8,128)(2,1)}, u32[]{:S(2)}, u32[]{:S(2)}) async-start(bf16[8,256,384]{2,1,0:T(8,128)(2,1)} %bitcast.167), calls=%async_computation.5 | async-start | bytes 3145728 | tf_op jit(solution)/shard_map/all_to_all | solution.py:659
  595.1 622.1 %all-gather.19.cloned.1.call-start = ((), (), s32[]{:S(2)}) async-start(), calls=%async_computation.12 | async-start | bytes 4456448 | tf_op jit(solution)/shard_map/all_gather | solution.py:622
  693.6 104.6 %collective-permute-start.53 = (bf16[256,1024]{1,0:T(8,128)(2,1)}, bf16[256,1024]{1,0:T(8,128)(2,1)}, u32[]{:S(2)}, u32[]{:S(2)}) collective-permute-start(bf16[256,1024]{1,0:T(8,128)(2,1)} %get-tuple-element.266.grad_ref.cols_ref), channel_id=1, source_target_pairs={{0,2},{2,0},{1,3},{3,1},{4,6},{6,4},{5,7},{7,5},{8,10},{10,8},{9,1... | collective-permute-start | bytes 1572872 | tf_op jit(solution)/shard_map/ppermute | solution.py:559
  749.7 53.8 %all-to-all-start.6 = ((bf16[8,256,128]{2,1,0:T(8,128)(2,1)}), bf16[8,256,128]{2,1,0:T(8,128)(2,1)}, u32[]{:S(2)}, u32[]{:S(2)}) async-start(bf16[8,256,128]{2,1,0:T(8,128)(2,1)} %shard_map.279), calls=%async_computation.6 | async-start | bytes 1048576 | tf_op jit(solution)/shard_map/all_to_all | solution.py:659
  753.9 469.9 %all-gather.17.cloned.1.call-start = ((), (), s32[]{:S(2)}) async-start(), calls=%async_computation.11 | async-start | bytes 4456448 | tf_op jit(solution)/shard_map/all_gather | solution.py:622
  783.3 108.6 %collective-permute-start.37 = (bf16[256,512]{1,0:T(8,128)(2,1)}, bf16[256,512]{1,0:T(8,128)(2,1)}, u32[]{:S(2)}, u32[]{:S(2)}) collective-permute-start(bf16[256,512]{1,0:T(8,128)(2,1)} %pad_maximum_fusion.15), channel_id=1, source_target_pairs={{0,2},{2,0},{1,3},{3,1},{4,6},{6,4},{5,7},{7,5},{8,10},{10,8},{9,1... | collective-permute-start | bytes 786440 | tf_op jit(solution)/shard_map/ppermute | solution.py:559
  868.1 75.6 %all-to-all-start.7 = ((bf16[8,256,384]{2,1,0:T(8,128)(2,1)}), bf16[8,256,384]{2,1,0:T(8,128)(2,1)}, u32[]{:S(2)}, u32[]{:S(2)}) async-start(bf16[8,256,384]{2,1,0:T(8,128)(2,1)} %bitcast.166), calls=%async_computation.7 | async-start | bytes 3145728 | tf_op jit(solution)/shard_map/all_to_all | solution.py:659
  872.4 358.1 %all-gather.15.cloned.1.call-start = ((), (), s32[]{:S(2)}) async-start(), calls=%async_computation.10 | async-start | bytes 4456448 | tf_op jit(solution)/shard_map/all_gather | solution.py:622
  883.3 54.6 %collective-permute-start.77 = (bf16[256,2048]{1,0:T(8,128)(2,1)}, bf16[256,2048]{1,0:T(8,128)(2,1)}, u32[]{:S(2)}, u32[]{:S(2)}) collective-permute-start(bf16[256,2048]{1,0:T(8,128)(2,1)} %shard_map.316), channel_id=1, source_target_pairs={{0,1},{1,0},{2,3},{3,2},{4,5},{5,4},{6,7},{7,6},{8,9},{9,8},{10,11... | collective-permute-start | bytes 3145736 | tf_op jit(solution)/shard_map/ppermute | solution.py:559
  889.3 82.2 %collective-permute-start.51 = (bf16[256,3072]{1,0:T(8,128)(2,1)}, bf16[256,3072]{1,0:T(8,128)(2,1)S(1)}, u32[]{:S(2)}, u32[]{:S(2)}) collective-permute-start(bf16[256,3072]{1,0:T(8,128)(2,1)} %shard_map.291), channel_id=1, source_target_pairs={{0,1},{1,0},{2,3},{3,2},{4,5},{5,4},{6,7},{7,6},{8,9},{9,8},{10,11... | collective-permute-start | bytes 4718600 | tf_op jit(solution)/shard_map/ppermute | solution.py:559
  891.9 114.3 %collective-permute-start.24 = (bf16[256,512]{1,0:T(8,128)(2,1)}, bf16[256,512]{1,0:T(8,128)(2,1)S(1)}, u32[]{:S(2)}, u32[]{:S(2)}) collective-permute-start(bf16[256,512]{1,0:T(8,128)(2,1)} %pad_maximum_fusion.14), channel_id=1, source_target_pairs={{0,2},{2,0},{1,3},{3,1},{4,6},{6,4},{5,7},{7,5},{8,10},{10,8},{9,1... | collective-permute-start | bytes 786440 | tf_op jit(solution)/shard_map/ppermute | solution.py:559
  896.0 113.7 %collective-permute-start.39 = (bf16[256,1024]{1,0:T(8,128)(2,1)}, bf16[256,1024]{1,0:T(8,128)(2,1)}, u32[]{:S(2)}, u32[]{:S(2)}) collective-permute-start(bf16[256,1024]{1,0:T(8,128)(2,1)} %shard_map.286), channel_id=1, source_target_pairs={{0,1},{1,0},{2,3},{3,2},{4,5},{5,4},{6,7},{7,6},{8,9},{9,8},{10,11... | collective-permute-start | bytes 1572872 | tf_op jit(solution)/shard_map/ppermute | solution.py:559
  1069.6 72.6 %collective-permute-start.86 = (bf16[4,32,4096]{2,1,0:T(8,128)(2,1)}, bf16[4,32,4096]{2,1,0:T(8,128)(2,1)}, u32[]{:S(2)}, u32[]{:S(2)}) collective-permute-start(bf16[4,32,4096]{2,1,0:T(8,128)(2,1)} %get-tuple-element.301), channel_id=1, source_target_pairs={{0,4},{4,0},{1,5},{5,1},{2,6},{6,2},{3,7},{7,3},{8,12},{12,8},{9,1... | collective-permute-start | bytes 3145736 | tf_op jit(solution)/shard_map/ppermute | solution.py:559
  (174 other events, 2903.0 us)
Sparse Core Ops, SparseCore 0:
  20.9 57.2 all-gather.10
  127.4 62.0 all-gather.12
  479.9 53.6 all-gather.20
  640.9 56.7 all-gather.18
  798.2 55.4 all-gather.16
  1053.4 67.4 all-gather.14

commit v2 on v1

--- a/solution.py
+++ b/solution.py
@@ -13,7 +13,7 @@
 GROUP = 8
 LANES = 128
 KEYS = 1536
-KEYS_BACK = 768
+KEYS_BACK = 1536
 BF = jnp.bfloat16
 F32 = jnp.float32
 ALL = ("z", "y", "c", "x")
@@ -21,9 +21,9 @@
 QKV, OUT, FC1, FC2 = range(4)
 UNITS = ((QKV, 0, 3), (QKV, 0, 1), (QKV, 1, 2), (OUT, 0, 1), (FC1, 0, 2), (FC1, 2, 2), (FC2, 0, 2), (FC2, 2, 2))
 NQKV, NQ, NKV, NOUT, FC1A, FC1B, FC2A, FC2B = range(8)
-GROUPS = ((NOUT, NQKV), (FC1A, FC1B), (FC2A, FC2B), (NOUT, NQ), (NKV,))
-GQ, G1, G2, GA, GB = range(5)
-USED = ((G2, G1, GA, GB), (G2, G1, GQ))
+GROUPS = ((FC1A, FC1B, NOUT, NQKV), (FC1A, FC1B), (FC2A, FC2B), (NOUT, NQ), (NKV,))
+GM, G1, G2, GA, GB = range(5)
+USED = ((G2, G1, GA, GB), (G2, GM))
 BY_HAND = ((G2, 0), (GA, 0), (GB, 0))
 
 
@@ -664,7 +664,7 @@
         return swap_group(blocks.reshape(GROUP * count, kinds * (width // GROUP)))
 
     def to_tokens(heads, kinds):
-        swapped = lax.all_to_all(heads, group_axes, split_axis=0, concat_axis=0, tiled=True)
+        swapped = swap_group(heads)
         count = heads.shape[0] // GROUP
         blocks = swapped.reshape(GROUP, count, kinds, heads.shape[1] // kinds)
         return blocks.transpose(1, 2, 0, 3).reshape(count, kinds * GROUP * (heads.shape[1] // kinds))
@@ -871,12 +871,16 @@
                     w_qkv, layer, [(w, half // 2, 0) for w in first_w], qkv_starts, width,
                     [whole_row(width), col_block(width)], [kind((count, width), F32), kind((count, 3 * width), BF)],
                 )
-                firsts |= grad_first(normed_in, partner[QKV], g_proj, (NQKV,) if GQ in USED[layer] else (NQ, NKV), spot)
+                firsts |= grad_first(normed_in, partner[QKV], g_proj, (NQKV,) if GM in USED[layer] else (NQ, NKV), spot)
                 out_span, qkv_wide = (0, 1, width, None), 3 * width
                 spans = {
                     G2: ((FC2, (0, fc2_subs, width, None)),),
                     G1: ((FC1, (0, 1, hidden_size, None)),),
-                    GQ: ((OUT, out_span), (QKV, (width, 1, qkv_wide, None))),
+                    GM: (
+                        (FC1, (0, 1, hidden_size, None)),
+                        (OUT, (hidden_size, 1, width, None)),
+                        (QKV, (hidden_size + width, 1, qkv_wide, None)),
+                    ),
                     GA: ((OUT, out_span), (QKV, (width, 1, qkv_wide, 0))),
                     GB: ((QKV, (0, 1, qkv_wide, 1)),),
                 }

time: 1280 us -> 1340 us (1.047)
  waiting for transfers between devices: 527 us -> 605 us
  starting transfers between devices: 170 us -> 155 us
    ppermute x91 -> x87, waiting for transfers between devices: 407 us -> 491 us  [flip(): return lax.ppermute(value, axis, [(i, i ^ bit) for i in range(sizes[axis])])]
    all_to_all x5 -> x7, waiting for transfers between devices: 32.9 us -> 54 us  [swap_group(): lax.all_to_all(blocks, group_axes, split_axis=0, concat_axis=0, tiled=True)]
    ppermute x91 -> x87, starting transfers between devices: 109 us -> 89.9 us  [flip(): return lax.ppermute(value, axis, [(i, i ^ bit) for i in range(sizes[axis])])]
    all_to_all x2 -> x0, waiting for transfers between devices: 16.3 us -> none  [to_tokens(): lax.all_to_all(heads, group_axes, split_axis=0, concat_axis=0, tiled=True)]
    all_to_all x5 -> x7, starting transfers between devices: 21.2 us -> 27.2 us  [swap_group(): lax.all_to_all(blocks, group_axes, split_axis=0, concat_axis=0, tiled=True)]
    pallas_call x10 -> x9, Pallas kernels: 49.4 us -> 46.3 us  [place_rows(): pl.pallas_call(lambda *refs: place_kernel(spans, z_major, *refs), grid_sp...]
  transfers between devices with their start and end apart: 114 -> 109, of which waited for: 48 -> 45; matrix products, arithmetic and copies ran while one was open for 7% -> 7% of each run, Pallas kernels for 31% -> 30%
where the time goes in v2:
time: 1340 us; the launch traced here: 1320 us
  waiting for transfers between devices  605 us (45%)
  Pallas kernels  401 us (30%)
  starting transfers between devices  155 us (12%)
  other arithmetic  68.9 us (5%)
  local copies, waits for them, and re-layouts  53.3 us (4%)
  blocking collectives  23.9 us (2%)
  between operations  16.3 us (1%)
    ppermute x87, waiting for transfers between devices, flip(): return lax.ppermute(value, axis, [(i, i ^ bit) for i in range(sizes[axis])])  491 us
    pallas_call x26, Pallas kernels, block_grad(): pl.pallas_call(kernel, grid_spec=pltpu.PrefetchScalarGridSpec(num_scalar_...  103 us
    ppermute x87, starting transfers between devices, flip(): return lax.ppermute(value, axis, [(i, i ^ bit) for i in range(sizes[axis])])  89.9 us
    pallas_call x2, Pallas kernels, attn_bwd(): pl.pallas_call(attn_bwd_kernel, grid_spec=pltpu.PrefetchScalarGridSpec(nu...  63.7 us
    ppermute x10, waiting for transfers between devices, shift_groups(): return lax.ppermute(value, ALL, pairs)  60.2 us
    pallas_call x8, Pallas kernels, product(): pl.pallas_call(kernel, grid_spec=pltpu.PrefetchScalarGridSpec(num_scalar_...  57.5 us
    all_to_all x7, waiting for transfers between devices, swap_group(): lax.all_to_all(blocks, group_axes, split_axis=0, concat_axis=0, tiled=True)  54 us
    pallas_call x9, Pallas kernels, place_rows(): pl.pallas_call(lambda *refs: place_kernel(spans, z_major, *refs), grid_sp...  46.3 us
  transfers between devices with their start and end apart: 109, of which 45 were waited for; matrix products, arithmetic and copies ran while one was open for 7% of the time, Pallas kernels for 30%

profile of v2, /device:TPU:0, one launch (start us, length us, event | category | flops | bytes accessed | tf_op | source)
XLA Modules:
  0.0 1323.4 jit_solution(13445005718277118770)
XLA Ops:
  40.9 23.5 %collective-permute-done.6.refs_0_ = bf16[256,3072]{1,0:T(8,128)(2,1)S(1)} collective-permute-done((bf16[256,3072]{1,0:T(8,128)(2,1)}, bf16[256,3072]{1,0:T(8,128)(2,1)S(1)}, u32[]{:S(2)}, u32[]{:S(2)}) %collective-permute-start.6) | collective-permute-done | bytes 1572896 | tf_op jit(solution)/shard_map/ppermute | solution.py:559
  88.1 62.0 %collective-permute-done.17 = bf16[32,5120]{1,0:T(8,128)(2,1)S(1)} collective-permute-done((bf16[32,5120]{1,0:T(8,128)(2,1)S(1)}, bf16[32,5120]{1,0:T(8,128)(2,1)S(1)}, u32[]{:S(2)}, u32[]{:S(2)}) %collective-permute-start.17) | collective-permute-done | bytes 327712 | tf_op jit(solution)/shard_map/ppermute | solution.py:559
  170.6 29.2 %collective-permute-done.9 = bf16[1536,256]{1,0:T(8,128)(2,1)S(1)} collective-permute-done((bf16[1536,256]{1,0:T(8,128)(2,1)S(1)}, bf16[1536,256]{1,0:T(8,128)(2,1)S(1)}, u32[]{:S(2)}, u32[]{:S(2)}) %collective-permute-start.9) | collective-permute-done | bytes 786464 | tf_op jit(solution)/shard_map/ppermute | solution.py:563
  201.5 18.5 %attn_fwd.2 = (bf16[2048,128]{1,0:T(8,128)(2,1)}, f32[2048,128]{1,0:T(8,128)}, f32[8,1,512]{2,1,0:T(1,128)}) custom-call(s32[8]{0:T(128)} %get-tuple-element.352.lo_ref, s32[8]{0:T(128)} %get-tuple-element.353.hi_ref, bf16[2048,384]{1,0:T(8,128)(2,1)} %bitcast.151, bf16[5120,256]{1,0:T(8,128)(2,1)} %pad_maximum_fusion.k_ref.v_ref, ...), custom_call_target="tpu_custom_call" | custom-call | flops 3758096384 | bytes 4718592 | tf_op jit(solution)/shard_map/attn_fwd/pallas_call | solution.py:119
  268.1 23.9 %all_to_all.68 = bf16[8,256,384]{2,1,0:T(8,128)(2,1)S(1)} all-to-all(bf16[8,256,384]{2,1,0:T(8,128)(2,1)} %shard_map.260), channel_id=1, replica_groups=mesh['z'=4,'y'=2,'c'=2,'x'=2] {'y','c','x'}, dimensions={0} | all-to-all | bytes 3145728 | tf_op jit(solution)/shard_map/all_to_all | solution.py:659
  299.6 13.9 %collective-permute-done.16 = bf16[1536,256]{1,0:T(8,128)(2,1)S(1)} collective-permute-done((bf16[1536,256]{1,0:T(8,128)(2,1)S(1)}, bf16[1536,256]{1,0:T(8,128)(2,1)S(1)}, u32[]{:S(2)}, u32[]{:S(2)}) %collective-permute-start.16) | collective-permute-done | bytes 786464 | tf_op jit(solution)/shard_map/ppermute | solution.py:563
  316.4 18.5 %attn_fwd.3 = (bf16[2048,128]{1,0:T(8,128)(2,1)}, f32[2048,128]{1,0:T(8,128)}, f32[8,1,512]{2,1,0:T(1,128)}) custom-call(s32[8]{0:T(128)} %get-tuple-element.352.lo_ref, s32[8]{0:T(128)} %get-tuple-element.353.hi_ref, bf16[2048,384]{1,0:T(8,128)(2,1)} %bitcast.155, bf16[5120,256]{1,0:T(8,128)(2,1)} %pad_maximum_fusion.1.k_ref.v_ref, ...), custom_call_target="tpu_custom_call" | custom-call | flops 3758096384 | bytes 4718592 | tf_op jit(solution)/shard_map/attn_fwd/pallas_call | solution.py:119
  418.2 28.3 %collective-permute-done.87.came_ref = bf16[256,2048]{1,0:T(8,128)(2,1)} collective-permute-done((bf16[256,2048]{1,0:T(8,128)(2,1)}, bf16[256,2048]{1,0:T(8,128)(2,1)}, u32[]{:S(2)}, u32[]{:S(2)}) %collective-permute-start.87) | collective-permute-done | bytes 1048608 | tf_op jit(solution)/shard_map/ppermute | solution.py:559
  456.4 31.7 %attn_bwd.2 = (bf16[2048,128]{1,0:T(8,128)(2,1)}, f32[2048,256]{1,0:T(8,128)}, bf16[1536,256]{1,0:T(8,128)(2,1)}, bf16[1536,256]{1,0:T(8,128)(2,1)}) custom-call(s32[8]{0:T(128)} %get-tuple-element.352.lo_ref, s32[8]{0:T(128)} %get-tuple-element.353.hi_ref, bf16[2048,384]{1,0:T(8,128)(2,1)} %bitcast.156, bf16[5120,256]{1,0:T(8,128)(2,1)} %pad_maximum_fusion.1.k_ref.v_ref, ...), custom_call_target="tpu_custom_call" | custom-call | flops 9395240960 | bytes 11010048 | tf_op jit(solution)/shard_map/attn_bwd/pallas_call | solution.py:216
  506.0 18.5 %collective-permute-done.89.refs_1_ = bf16[32,4096]{1,0:T(8,128)(2,1)S(1)} collective-permute-done((bf16[32,4096]{1,0:T(8,128)(2,1)}, bf16[32,4096]{1,0:T(8,128)(2,1)S(1)}, u32[]{:S(2)}, u32[]{:S(2)}) %collective-permute-start.89) | collective-permute-done | bytes 262176 | tf_op jit(solution)/shard_map/ppermute | solution.py:559
  545.9 22.2 %all-to-all-done.5.heads_ref = bf16[8,256,384]{2,1,0:T(8,128)(2,1)} async-done(((bf16[8,256,384]{2,1,0:T(8,128)(2,1)}), bf16[8,256,384]{2,1,0:T(8,128)(2,1)}, u32[]{:S(2)}, u32[]{:S(2)}) %all-to-all-start.5) | async-done | bytes 1572896 | tf_op jit(solution)/shard_map/all_to_all | solution.py:659
  608.7 37.9 %collective-permute-done.58.came_ref = bf16[256,2048]{1,0:T(8,128)(2,1)} collective-permute-done((bf16[256,2048]{1,0:T(8,128)(2,1)}, bf16[256,2048]{1,0:T(8,128)(2,1)}, u32[]{:S(2)}, u32[]{:S(2)}) %collective-permute-start.58) | collective-permute-done | bytes 1048608 | tf_op jit(solution)/shard_map/ppermute | solution.py:559
  650.7 18.4 %collective-permute-done.57.came_ref = bf16[256,2048]{1,0:T(8,128)(2,1)} collective-permute-done((bf16[256,2048]{1,0:T(8,128)(2,1)}, bf16[256,2048]{1,0:T(8,128)(2,1)}, u32[]{:S(2)}, u32[]{:S(2)}) %collective-permute-start.57) | collective-permute-done | bytes 1048608 | tf_op jit(solution)/shard_map/ppermute | solution.py:559
  689.7 46.6 %collective-permute-done.59.came_ref = bf16[128,8192]{1,0:T(8,128)(2,1)S(1)} collective-permute-done((bf16[128,8192]{1,0:T(8,128)(2,1)}, bf16[128,8192]{1,0:T(8,128)(2,1)S(1)}, u32[]{:S(2)}, u32[]{:S(2)}) %collective-permute-start.59) | collective-permute-done | bytes 2097184 | tf_op jit(solution)/shard_map/ppermute | solution.py:559
  747.9 17.3 %collective-permute-done.60.refs_1_ = bf16[32,8192]{1,0:T(8,128)(2,1)S(1)} collective-permute-done((bf16[32,8192]{1,0:T(8,128)(2,1)}, bf16[32,8192]{1,0:T(8,128)(2,1)S(1)}, u32[]{:S(2)}, u32[]{:S(2)}) %collective-permute-start.60) | collective-permute-done | bytes 524320 | tf_op jit(solution)/shard_map/ppermute | solution.py:559
  765.3 18.6 %collective-permute-done.61.refs_2_ = bf16[32,8192]{1,0:T(8,128)(2,1)S(1)} collective-permute-done((bf16[32,8192]{1,0:T(8,128)(2,1)}, bf16[32,8192]{1,0:T(8,128)(2,1)S(1)}, u32[]{:S(2)}, u32[]{:S(2)}) %collective-permute-start.61) | collective-permute-done | bytes 524320 | tf_op jit(solution)/shard_map/ppermute | solution.py:559
  845.7 32.0 %attn_bwd.3 = (bf16[2048,128]{1,0:T(8,128)(2,1)}, f32[2048,256]{1,0:T(8,128)}, bf16[1536,256]{1,0:T(8,128)(2,1)}, bf16[1536,256]{1,0:T(8,128)(2,1)}) custom-call(s32[8]{0:T(128)} %get-tuple-element.352.lo_ref, s32[8]{0:T(128)} %get-tuple-element.353.hi_ref, bf16[2048,384]{1,0:T(8,128)(2,1)} %bitcast.152, bf16[5120,256]{1,0:T(8,128)(2,1)} %pad_maximum_fusion.k_ref.v_ref, ...), custom_call_target="tpu_custom_call" | custom-call | flops 9395240960 | bytes 11010048 | tf_op jit(solution)/shard_map/attn_bwd/pallas_call | solution.py:216
  943.7 18.3 %collective-permute-done.74.came_ref = bf16[256,2048]{1,0:T(8,128)(2,1)} collective-permute-done((bf16[256,2048]{1,0:T(8,128)(2,1)}, bf16[256,2048]{1,0:T(8,128)(2,1)}, u32[]{:S(2)}, u32[]{:S(2)}) %collective-permute-start.74) | collective-permute-done | bytes 1048608 | tf_op jit(solution)/shard_map/ppermute | solution.py:559
  966.2 18.4 %collective-permute-done.73.came_ref = bf16[256,2048]{1,0:T(8,128)(2,1)} collective-permute-done((bf16[256,2048]{1,0:T(8,128)(2,1)}, bf16[256,2048]{1,0:T(8,128)(2,1)}, u32[]{:S(2)}, u32[]{:S(2)}) %collective-permute-start.73) | collective-permute-done | bytes 1048608 | tf_op jit(solution)/shard_map/ppermute | solution.py:559
  1002.2 15.9 %collective-permute-done.66.came_ref = bf16[256,2048]{1,0:T(8,128)(2,1)S(1)} collective-permute-done((bf16[256,2048]{1,0:T(8,128)(2,1)}, bf16[256,2048]{1,0:T(8,128)(2,1)S(1)}, u32[]{:S(2)}, u32[]{:S(2)}) %collective-permute-start.66) | collective-permute-done | bytes 1048608 | tf_op jit(solution)/shard_map/ppermute | solution.py:559
  1023.4 16.7 %collective-permute-done.65.came_ref = bf16[256,2048]{1,0:T(8,128)(2,1)S(1)} collective-permute-done((bf16[256,2048]{1,0:T(8,128)(2,1)}, bf16[256,2048]{1,0:T(8,128)(2,1)S(1)}, u32[]{:S(2)}, u32[]{:S(2)}) %collective-permute-start.65) | collective-permute-done | bytes 1048608 | tf_op jit(solution)/shard_map/ppermute | solution.py:559
  1053.7 16.6 %collective-permute-done.67.came_ref = bf16[128,4096]{1,0:T(8,128)(2,1)} collective-permute-done((bf16[128,4096]{1,0:T(8,128)(2,1)}, bf16[128,4096]{1,0:T(8,128)(2,1)}, u32[]{:S(2)}, u32[]{:S(2)}) %collective-permute-start.67) | collective-permute-done | bytes 1048608 | tf_op jit(solution)/shard_map/ppermute | solution.py:559
  1138.4 15.2 %collective-permute-done.36.came_ref = bf16[256,1024]{1,0:T(8,128)(2,1)} collective-permute-done((bf16[256,1024]{1,0:T(8,128)(2,1)}, bf16[256,1024]{1,0:T(8,128)(2,1)}, u32[]{:S(2)}, u32[]{:S(2)}) %collective-permute-start.36) | collective-permute-done | bytes 524320 | tf_op jit(solution)/shard_map/ppermute | solution.py:559
  1214.5 14.6 %collective-permute-done.29.refs_2_ = bf16[32,2048]{1,0:T(8,128)(2,1)S(1)} collective-permute-done((bf16[32,2048]{1,0:T(8,128)(2,1)}, bf16[32,2048]{1,0:T(8,128)(2,1)S(1)}, u32[]{:S(2)}, u32[]{:S(2)}) %collective-permute-start.29) | collective-permute-done | bytes 131104 | tf_op jit(solution)/shard_map/ppermute | solution.py:559
  (711 shorter events, 730.3 us)
Async XLA Ops:
  7.3 226.5 %all-gather.9.cloned.1.call-start = ((), (), s32[]{:S(2)}) async-start(), calls=%async_computation.8 | async-start | bytes 5570560 | tf_op jit(solution)/shard_map/all_gather | solution.py:583
  33.6 136.2 %collective-permute-start.11 = (bf16[1024,1024]{1,0:T(8,128)(2,1)}, bf16[1024,1024]{1,0:T(8,128)(2,1)}, u32[]{:S(2)}, u32[]{:S(2)}) collective-permute-start(bf16[1024,1024]{1,0:T(8,128)(2,1)} %get-tuple-element.276), channel_id=1, source_target_pairs={{0,1},{1,0},{2,3},{3,2},{4,5},{5,4},{6,7},{7,6},{8,9},{9,8},{10,11... | collective-permute-start | bytes 6291464 | tf_op jit(solution)/shard_map/ppermute | solution.py:559
  33.7 190.4 %collective-permute-start.13 = (bf16[256,3072]{1,0:T(8,128)(2,1)}, bf16[256,3072]{1,0:T(8,128)(2,1)}, u32[]{:S(2)}, u32[]{:S(2)}) collective-permute-start(bf16[256,3072]{1,0:T(8,128)(2,1)} %get-tuple-element.279), channel_id=1, source_target_pairs={{0,1},{1,0},{2,3},{3,2},{4,5},{5,4},{6,7},{7,6},{8,9},{9,8},{10,11... | collective-permute-start | bytes 4718600 | tf_op jit(solution)/shard_map/ppermute | solution.py:559
  38.7 111.4 %collective-permute-start.17 = (bf16[32,5120]{1,0:T(8,128)(2,1)S(1)}, bf16[32,5120]{1,0:T(8,128)(2,1)S(1)}, u32[]{:S(2)}, u32[]{:S(2)}) collective-permute-start(bf16[32,5120]{1,0:T(8,128)(2,1)S(1)} %pad_maximum_fusion.13), channel_id=1, source_target_pairs={{0,1},{1,0},{2,3},{3,2},{4,5},{5,4},{6,7},{7,6},{8,9},{9,8},{10,11... | collective-permute-start | bytes 983048 | tf_op jit(solution)/shard_map/ppermute | solution.py:559
  75.5 88.3 %all-to-all-start = ((bf16[8,256,384]{2,1,0:T(8,128)(2,1)}), bf16[8,256,384]{2,1,0:T(8,128)(2,1)S(1)}, u32[]{:S(2)}, u32[]{:S(2)}) async-start(bf16[8,256,384]{2,1,0:T(8,128)(2,1)} %shard_map.256), calls=%async_computation | async-start | bytes 3145728 | tf_op jit(solution)/shard_map/all_to_all | solution.py:659
  79.5 272.2 %all-gather.11.cloned.1.call-start = ((), (), s32[]{:S(2)}) async-start(), calls=%async_computation.9 | async-start | bytes 5570560 | tf_op jit(solution)/shard_map/all_gather | solution.py:583
  169.9 81.4 %collective-permute-start.12 = (bf16[1024,1024]{1,0:T(8,128)(2,1)}, bf16[1024,1024]{1,0:T(8,128)(2,1)}, u32[]{:S(2)}, u32[]{:S(2)}) collective-permute-start(bf16[1024,1024]{1,0:T(8,128)(2,1)} %collective-permute-done.11.refs_0_), channel_id=1, source_target_pairs={{0,2},{2,0},{1,3},{3,1},{4,6},{6,4},{5,7},{7,5},{8,10},{10,8},{9,1... | collective-permute-start | bytes 6291464 | tf_op jit(solution)/shard_map/ppermute | solution.py:559
  397.7 52.9 %collective-permute-start.86 = (bf16[256,2048]{1,0:T(8,128)(2,1)}, bf16[256,2048]{1,0:T(8,128)(2,1)}, u32[]{:S(2)}, u32[]{:S(2)}) collective-permute-start(bf16[256,2048]{1,0:T(8,128)(2,1)} %shard_map.310), channel_id=1, source_target_pairs={{0,1},{1,0},{2,3},{3,2},{4,5},{5,4},{6,7},{7,6},{8,9},{9,8},{10,11... | collective-permute-start | bytes 3145736 | tf_op jit(solution)/shard_map/ppermute | solution.py:559
  414.7 854.4 %all-gather.17.cloned.1.call-start = ((), (), s32[]{:S(2)}) async-start(), calls=%async_computation.12 | async-start | bytes 4456448 | tf_op jit(solution)/shard_map/all_gather | solution.py:622
  545.2 738.6 %all-gather.13.cloned.1.call-start = ((), (), s32[]{:S(2)}) async-start(), calls=%async_computation.10 | async-start | bytes 8912896 | tf_op jit(solution)/shard_map/all_gather | solution.py:622
  586.5 97.0 %collective-permute-start.51 = (bf16[256,3072]{1,0:T(8,128)(2,1)}, bf16[256,3072]{1,0:T(8,128)(2,1)}, u32[]{:S(2)}, u32[]{:S(2)}) collective-permute-start(bf16[256,3072]{1,0:T(8,128)(2,1)} %shard_map.282), channel_id=1, source_target_pairs={{0,1},{1,0},{2,3},{3,2},{4,5},{5,4},{6,7},{7,6},{8,9},{9,8},{10,11... | collective-permute-start | bytes 4718600 | tf_op jit(solution)/shard_map/ppermute | solution.py:559
  594.9 51.6 %collective-permute-start.58 = (bf16[256,2048]{1,0:T(8,128)(2,1)}, bf16[256,2048]{1,0:T(8,128)(2,1)}, u32[]{:S(2)}, u32[]{:S(2)}) collective-permute-start(bf16[256,2048]{1,0:T(8,128)(2,1)} %shard_map.285), channel_id=1, source_target_pairs={{0,1},{1,0},{2,3},{3,2},{4,5},{5,4},{6,7},{7,6},{8,9},{9,8},{10,11... | collective-permute-start | bytes 3145736 | tf_op jit(solution)/shard_map/ppermute | solution.py:559
  599.5 69.5 %collective-permute-start.57 = (bf16[256,2048]{1,0:T(8,128)(2,1)}, bf16[256,2048]{1,0:T(8,128)(2,1)}, u32[]{:S(2)}, u32[]{:S(2)}) collective-permute-start(bf16[256,2048]{1,0:T(8,128)(2,1)} %shard_map.284), channel_id=1, source_target_pairs={{0,1},{1,0},{2,3},{3,2},{4,5},{5,4},{6,7},{7,6},{8,9},{9,8},{10,11... | collective-permute-start | bytes 3145736 | tf_op jit(solution)/shard_map/ppermute | solution.py:559
  607.9 71.4 %collective-permute-start.54 = (bf16[256,1024]{1,0:T(8,128)(2,1)}, bf16[256,1024]{1,0:T(8,128)(2,1)S(1)}, u32[]{:S(2)}, u32[]{:S(2)}) collective-permute-start(bf16[256,1024]{1,0:T(8,128)(2,1)} %shard_map.283), channel_id=1, source_target_pairs={{0,1},{1,0},{2,3},{3,2},{4,5},{5,4},{6,7},{7,6},{8,9},{9,8},{10,11... | collective-permute-start | bytes 1572872 | tf_op jit(solution)/shard_map/ppermute | solution.py:559
  834.5 95.2 %collective-permute-start.37 = (bf16[256,512]{1,0:T(8,128)(2,1)}, bf16[256,512]{1,0:T(8,128)(2,1)S(1)}, u32[]{:S(2)}, u32[]{:S(2)}) collective-permute-start(bf16[256,512]{1,0:T(8,128)(2,1)} %pad_maximum_fusion.15), channel_id=1, source_target_pairs={{0,2},{2,0},{1,3},{3,1},{4,6},{6,4},{5,7},{7,5},{8,10},{10,8},{9,1... | collective-permute-start | bytes 786440 | tf_op jit(solution)/shard_map/ppermute | solution.py:559
  914.5 75.7 %all-to-all-start.7 = ((bf16[8,256,384]{2,1,0:T(8,128)(2,1)}), bf16[8,256,384]{2,1,0:T(8,128)(2,1)}, u32[]{:S(2)}, u32[]{:S(2)}) async-start(bf16[8,256,384]{2,1,0:T(8,128)(2,1)} %bitcast.166), calls=%async_computation.7 | async-start | bytes 3145728 | tf_op jit(solution)/shard_map/all_to_all | solution.py:659
  919.0 385.6 %all-gather.15.cloned.1.call-start = ((), (), s32[]{:S(2)}) async-start(), calls=%async_computation.11 | async-start | bytes 4456448 | tf_op jit(solution)/shard_map/all_gather | solution.py:622
  929.4 55.1 %collective-permute-start.73 = (bf16[256,2048]{1,0:T(8,128)(2,1)}, bf16[256,2048]{1,0:T(8,128)(2,1)}, u32[]{:S(2)}, u32[]{:S(2)}) collective-permute-start(bf16[256,2048]{1,0:T(8,128)(2,1)} %shard_map.304), channel_id=1, source_target_pairs={{0,1},{1,0},{2,3},{3,2},{4,5},{5,4},{6,7},{7,6},{8,9},{9,8},{10,11... | collective-permute-start | bytes 3145736 | tf_op jit(solution)/shard_map/ppermute | solution.py:559
  930.4 143.0 %collective-permute-start.24 = (bf16[256,512]{1,0:T(8,128)(2,1)}, bf16[256,512]{1,0:T(8,128)(2,1)S(1)}, u32[]{:S(2)}, u32[]{:S(2)}) collective-permute-start(bf16[256,512]{1,0:T(8,128)(2,1)} %pad_maximum_fusion.14), channel_id=1, source_target_pairs={{0,2},{2,0},{1,3},{3,1},{4,6},{6,4},{5,7},{7,5},{8,10},{10,8},{9,1... | collective-permute-start | bytes 786440 | tf_op jit(solution)/shard_map/ppermute | solution.py:559
  933.7 140.3 %collective-permute-start.39 = (bf16[256,1024]{1,0:T(8,128)(2,1)}, bf16[256,1024]{1,0:T(8,128)(2,1)}, u32[]{:S(2)}, u32[]{:S(2)}) collective-permute-start(bf16[256,1024]{1,0:T(8,128)(2,1)} %shard_map.277), channel_id=1, source_target_pairs={{0,1},{1,0},{2,3},{3,2},{4,5},{5,4},{6,7},{7,6},{8,9},{9,8},{10,11... | collective-permute-start | bytes 1572872 | tf_op jit(solution)/shard_map/ppermute | solution.py:559
  939.3 78.9 %collective-permute-start.66 = (bf16[256,2048]{1,0:T(8,128)(2,1)}, bf16[256,2048]{1,0:T(8,128)(2,1)S(1)}, u32[]{:S(2)}, u32[]{:S(2)}) collective-permute-start(bf16[256,2048]{1,0:T(8,128)(2,1)} %shard_map.298), channel_id=1, source_target_pairs={{0,1},{1,0},{2,3},{3,2},{4,5},{5,4},{6,7},{7,6},{8,9},{9,8},{10,11... | collective-permute-start | bytes 3145736 | tf_op jit(solution)/shard_map/ppermute | solution.py:559
  962.1 78.0 %collective-permute-start.65 = (bf16[256,2048]{1,0:T(8,128)(2,1)}, bf16[256,2048]{1,0:T(8,128)(2,1)S(1)}, u32[]{:S(2)}, u32[]{:S(2)}) collective-permute-start(bf16[256,2048]{1,0:T(8,128)(2,1)} %shard_map.297), channel_id=1, source_target_pairs={{0,1},{1,0},{2,3},{3,2},{4,5},{5,4},{6,7},{7,6},{8,9},{9,8},{10,11... | collective-permute-start | bytes 3145736 | tf_op jit(solution)/shard_map/ppermute | solution.py:559
  988.7 59.4 %collective-permute-start.75 = (bf16[128,4096]{1,0:T(8,128)(2,1)}, bf16[128,4096]{1,0:T(8,128)(2,1)}, u32[]{:S(2)}, u32[]{:S(2)}) collective-permute-start(bf16[128,4096]{1,0:T(8,128)(2,1)} %get-tuple-element.163), channel_id=1, source_target_pairs={{0,4},{4,0},{1,5},{5,1},{2,6},{6,2},{3,7},{7,3},{8,12},{12,8},{9,1... | collective-permute-start | bytes 3145736 | tf_op jit(solution)/shard_map/ppermute | solution.py:559
  1136.9 72.4 %collective-permute-start.82 = (bf16[4,32,4096]{2,1,0:T(8,128)(2,1)}, bf16[4,32,4096]{2,1,0:T(8,128)(2,1)}, u32[]{:S(2)}, u32[]{:S(2)}) collective-permute-start(bf16[4,32,4096]{2,1,0:T(8,128)(2,1)} %get-tuple-element.295), channel_id=1, source_target_pairs={{0,4},{4,0},{1,5},{5,1},{2,6},{6,2},{3,7},{7,3},{8,12},{12,8},{9,1... | collective-permute-start | bytes 3145736 | tf_op jit(solution)/shard_map/ppermute | solution.py:559
  (207 other events, 3509.7 us)
Sparse Core Ops, SparseCore 0:
  20.9 57.2 all-gather.8
  151.0 64.5 all-gather.10
  537.8 60.8 all-gather.16
  788.6 85.3 all-gather.12
  1120.7 65.8 all-gather.14
